TPU v7x, 512 devices: a whole 4x4x16 slice. The times are simulated.
512 devices in a mesh: shard: 128 (over z, y, core), tensor: 4 (over x).
Axes of the slice: x: 4, y: 4, z: 16, core: 2. Of those that a mesh axis runs over, the one named last changes fastest.
Arguments:
- wo_grads: bfloat16 [4, 2, 8, 8, 512, 512], P('tensor', None, None, None, 'shard'), may hold values from -6 to 6
- wo_master: float32 [2, 8, 8, 512, 512], P(None, None, None, 'shard', 'tensor'), may hold values from -0.09375 to 0.09375
- left_stats: float32 [256, 512, 512], P('shard', 'tensor'), may hold values from -6 to 6
- right_stats: float32 [256, 512, 512], P('shard', 'tensor'), may hold values from -6 to 6
- left_roots: bfloat16 [256, 512, 512], P('shard', 'tensor'), as said below
- right_roots: bfloat16 [256, 512, 512], P('shard', 'tensor'), as said below
- row_moments: float32 [256, 512], P('shard'), may hold values from 0.003 to 0.05
- col_moments: float32 [256, 512], P('shard'), may hold values from 0.002 to 0.1
- owners: int32 [128], replicated, may hold values from 0 to 127, as said below
- emb_grads: bfloat16 [4, 4096, 4096], P('tensor', 'shard'), may hold values from -3 to 3
- emb_master: float32 [4096, 4096], P('shard', 'tensor'), may hold values from -0.75 to 0.75
- emb_mean: float32 [4096, 4096], P('shard', 'tensor'), may hold values from -0.75 to 0.75
- emb_var: float32 [4096, 4096], P('shard', 'tensor'), may hold values from 0.002 to 0.05
- gain_grads: bfloat16 [4, 2, 4096], P('tensor', None, 'shard'), may hold values from -3 to 3
- gain_master: float32 [2, 4096], P(None, ('shard', 'tensor')), may hold values from 0.5 to 1.5
- gain_mean: float32 [2, 4096], P(None, ('shard', 'tensor')), may hold values from -0.75 to 0.75
- gain_var: float32 [2, 4096], P(None, ('shard', 'tensor')), may hold values from 0.002 to 0.05
Outputs:
- wo_new: float32 [2, 8, 8, 512, 512], P(None, None, None, 'shard', 'tensor')
- wo_weights: bfloat16 [2, 8, 8, 512, 512], P(None, None, None, 'shard')
- left_new: float32 [256, 512, 512], P('shard', 'tensor')
- right_new: float32 [256, 512, 512], P('shard', 'tensor')
- row_new: float32 [256, 512], P('shard')
- col_new: float32 [256, 512], P('shard')
- emb_new: float32 [4096, 4096], P('shard', 'tensor')
- emb_mean_new: float32 [4096, 4096], P('shard', 'tensor')
- emb_var_new: float32 [4096, 4096], P('shard', 'tensor')
- emb_weights: bfloat16 [4096, 4096], P('shard')
- gain_new: float32 [2, 4096], P(None, ('shard', 'tensor'))
- gain_mean_new: float32 [2, 4096], P(None, ('shard', 'tensor'))
- gain_var_new: float32 [2, 4096], P(None, ('shard', 'tensor'))
- gain_weights: bfloat16 [2, 4096], P(None, 'shard')
Inputs may be any that keep to these rules, and one draw needn't show every extreme that they name: `owners`: each index of shard owns at most 2 of the 128 blocks, and some index owns exactly 2. `left_roots`: each slot's matrix is symmetric. `right_roots`: each slot's matrix is symmetric.
All inputs are finite; a program needn't handle non-finite values.
Results may differ from a plain program's by a relative error of at most 0.0052.
Values may be sent and summed in bfloat16 or wider, within the bound.
No kernel may reach another device: no remote copies, remote signals or barrier semaphores. Data moves between devices by JAX's collectives and lax.ppermute only.
A program may use at most 128 MiB of HBM per device.

v0:
```python
import jax
import jax.numpy as jnp
from jax import lax
from jax.sharding import PartitionSpec as P

beta_one = 0.9
beta_two = 0.95
bias_one = 1.0 - 0.9**10
bias_two = 1.0 - 0.95**10
adam_eps = 1e-08
learn_rate = 0.01
decay_rate = 0.1
graft_eps = 1e-06
factor_eps = 1e-08
highest = lax.Precision.HIGHEST


def slot_table(owners, slot_count, owner_count):
    block_ids = jnp.arange(owners.shape[0], dtype=jnp.int32)
    earlier = (owners[:, None] == owners[None, :]) & (block_ids[None, :] < block_ids[:, None])
    owner_rank = jnp.sum(earlier.astype(jnp.int32), axis=1)
    slot_of = owners * slot_count + owner_rank
    slot_ids = jnp.arange(slot_count * owner_count, dtype=jnp.int32)
    slot_hits = (slot_of[:, None] == slot_ids[None, :]).astype(jnp.int32)
    block_of = jnp.sum(slot_hits * block_ids[:, None], axis=0)
    slot_used = jnp.sum(slot_hits, axis=0)
    return (slot_of, block_of, slot_used)


def adamw_step(gradient, master, first_moment, second_moment):
    mean_new = beta_one * first_moment + (1.0 - beta_one) * gradient
    var_new = beta_two * second_moment + (1.0 - beta_two) * gradient * gradient
    adam_dir = mean_new / bias_one / (jnp.sqrt(var_new / bias_two) + adam_eps)
    master_new = master - learn_rate * (adam_dir + decay_rate * master)
    return (master_new, mean_new, var_new, master_new.astype(jnp.bfloat16))


def per_device(
    wo_grads,
    wo_master,
    left_stats,
    right_stats,
    left_roots,
    right_roots,
    row_moments,
    col_moments,
    owners,
    emb_grads,
    emb_master,
    emb_mean,
    emb_var,
    gain_grads,
    gain_master,
    gain_mean,
    gain_var,
):
    micro_count = lax.axis_size("tensor")
    owner_count = lax.axis_size("shard")
    tensor_pos = lax.axis_index("tensor")
    slot_count = left_stats.shape[0]
    quarter = left_stats.shape[1]
    slot_of, block_of, slot_used = slot_table(owners, slot_count, owner_count)
    left_full = lax.all_gather(left_roots, "tensor", axis=1, tiled=True)
    emb_terms = emb_grads[0].astype(jnp.float32)
    gain_terms = gain_grads[0].astype(jnp.float32)
    wo_terms = wo_grads[0].astype(jnp.float32)
    wo_sum, emb_sum, gain_sum = (
        lax.psum_scatter(wo_terms, "tensor", scatter_dimension=4, tiled=True),
        lax.psum_scatter(emb_terms, "tensor", scatter_dimension=1, tiled=True),
        lax.psum_scatter(gain_terms, "tensor", scatter_dimension=1, tiled=True),
    )
    wo_mean = wo_sum / micro_count
    rows_dev = wo_mean.shape[3]
    flattened = wo_mean.reshape(-1, rows_dev, quarter)
    taken = jnp.take(flattened, block_of, axis=0)
    outgoing = jnp.where(slot_used[:, None, None] > 0, taken, 0.0)
    outgoing = outgoing.reshape(owner_count, slot_count, rows_dev, quarter)
    own_cols = lax.all_to_all(outgoing, "shard", split_axis=0, concat_axis=2, tiled=True)[0]
    full_block = lax.all_gather(own_cols, "tensor", axis=2, tiled=True)
    own_rows = lax.dynamic_slice_in_dim(full_block, tensor_pos * quarter, quarter, 1)
    left_new = left_stats + jnp.einsum("sqj,sij->sqi", own_rows, full_block, precision=highest)
    right_new = right_stats + jnp.einsum("siq,sij->sqj", own_cols, full_block, precision=highest)
    squares = full_block * full_block
    row_new = beta_two * row_moments + (1.0 - beta_two) * jnp.mean(squares, axis=2)
    col_new = beta_two * col_moments + (1.0 - beta_two) * jnp.mean(squares, axis=1)
    row_level = jnp.mean(row_new, axis=1)
    col_part = lax.dynamic_slice_in_dim(col_new, tensor_pos * quarter, quarter, 1)
    second_est = row_new[:, :, None] * col_part[:, None, :] / row_level[:, None, None]
    adam_dir = own_cols / (jnp.sqrt(second_est) + factor_eps)
    adam_part = jnp.sum(adam_dir * adam_dir, axis=(1, 2))
    adam_total = lax.psum(adam_part, "tensor")
    right_half = jnp.einsum(
        "sij,sqj->siq",
        full_block.astype(jnp.bfloat16),
        right_roots,
        preferred_element_type=jnp.float32,
    ).astype(jnp.bfloat16)
    shampoo = jnp.einsum("sik,skq->siq", left_full, right_half, preferred_element_type=jnp.float32)
    shampoo_part = jnp.sum(shampoo * shampoo, axis=(1, 2))
    shampoo_total = lax.psum(shampoo_part, "tensor")
    graft_ratio = jnp.sqrt(adam_total) / (jnp.sqrt(shampoo_total) + graft_eps)
    update = shampoo * graft_ratio[:, None, None]
    returned = lax.all_to_all(update, "shard", split_axis=1, concat_axis=0, tiled=True)
    local_update = jnp.take(returned, slot_of, axis=0).reshape(wo_master.shape)
    wo_new = wo_master - learn_rate * (local_update + decay_rate * wo_master)
    emb_grad = emb_sum / micro_count
    gain_grad = gain_sum / micro_count
    emb_new, emb_mean_new, emb_var_new, emb_low = adamw_step(
        emb_grad, emb_master, emb_mean, emb_var
    )
    gain_new, gain_mean_new, gain_var_new, gain_low = adamw_step(
        gain_grad, gain_master, gain_mean, gain_var
    )
    wo_weights, emb_weights, gain_weights = (
        lax.all_gather(wo_new.astype(jnp.bfloat16), "tensor", axis=4, tiled=True),
        lax.all_gather(emb_low, "tensor", axis=1, tiled=True),
        lax.all_gather(gain_low, "tensor", axis=1, tiled=True),
    )
    return (
        wo_new,
        wo_weights,
        left_new,
        right_new,
        row_new,
        col_new,
        emb_new,
        emb_mean_new,
        emb_var_new,
        emb_weights,
        gain_new,
        gain_mean_new,
        gain_var_new,
        gain_weights,
    )


def solution(mesh):
    in_specs = (
        P("tensor", None, None, None, "shard", None),
        P(None, None, None, "shard", "tensor"),
        P("shard", "tensor", None),
        P("shard", "tensor", None),
        P("shard", "tensor", None),
        P("shard", "tensor", None),
        P("shard", None),
        P("shard", None),
        P(),
        P("tensor", "shard", None),
        P("shard", "tensor"),
        P("shard", "tensor"),
        P("shard", "tensor"),
        P("tensor", None, "shard"),
        P(None, ("shard", "tensor")),
        P(None, ("shard", "tensor")),
        P(None, ("shard", "tensor")),
    )
    out_specs = (
        P(None, None, None, "shard", "tensor"),
        P(None, None, None, "shard", None),
        P("shard", "tensor", None),
        P("shard", "tensor", None),
        P("shard", None),
        P("shard", None),
        P("shard", "tensor"),
        P("shard", "tensor"),
        P("shard", "tensor"),
        P("shard", None),
        P(None, ("shard", "tensor")),
        P(None, ("shard", "tensor")),
        P(None, ("shard", "tensor")),
        P(None, "shard"),
    )
    return jax.shard_map(
        per_device, mesh=mesh, in_specs=in_specs, out_specs=out_specs, check_vma=False
    )
```

profile of v0, /device:TPU:40, one launch (start us, length us, event | category | flops | bytes accessed | tf_op | source)
XLA Modules:
  0.0 324.4 jit_solution(10380883053698371560)
XLA Ops:
  7.2 0.0 copy-start
  7.2 0.0 reduce-scatter.8.cloned.1.call-start
  7.2 1.2 bitcast_convert_fusion
  8.5 26.2 %copy.74 = f32[2,8,8,4,512]{3,2,1,0,4:T(8,128)} copy(f32[2,8,8,4,512]{4,3,2,1,0:T(4,128)S(1)} %bitcast_convert_fusion) | data formatting | bytes 2097152
  34.7 29.3 %reshape.124 = f32[512,512]{1,0:T(8,128)} reshape(f32[512,2,8,8,4]{4,3,2,1,0:T(8,128)} %bitcast.45) | data formatting | bytes 2097152
  64.0 0.0 reduce-scatter.8.cloned.1.call-update
  64.1 0.0 all-gather.4.cloned.1.call-start
  64.1 0.2 convert_reduce_fusion.1
  64.3 0.5 compare_and_fusion.1
  64.8 0.1 convert_reduce_fusion
  64.9 0.4 copy-done.12
  65.3 0.1 reduce_sum.79
  65.5 0.2 gt.18
  65.7 33.9 %reduce-scatter.8.cloned.1.call-done = f32[128,512]{1,0:T(8,128)} async-done(((f32[512,512]{1,0:T(8,128)}), f32[128,512]{1,0:T(8,128)}) %reduce-scatter.8.cloned.1.call-update) | async-done | bytes 262160
  99.6 10.8 %reshape.125 = f32[128,2,8,8,4]{4,3,2,1,0:T(8,128)} reshape(f32[128,512]{1,0:T(8,128)} %reduce-scatter.8.cloned.1.call-done) | data formatting | bytes 524288
  110.5 6.6 %copy.75 = f32[2,8,8,4,128]{4,3,2,1,0:T(4,128)S(1)} copy(f32[2,8,8,4,128]{3,2,1,0,4:T(8,128)} %bitcast.46) | data formatting | bytes 524288
  117.1 0.1 broadcast_multiply_fusion
  117.2 1.0 gather_fusion
  118.2 0.5 select_select_fusion
  118.7 0.0 copy-start.5
  118.8 0.2 copy.61
  118.9 0.0 copy-start.17
  119.0 48.5 %all_to_all.33 = f32[128,2,4,128]{3,1,2,0:T(2,128)S(1)} all-to-all(f32[128,2,4,128]{3,1,2,0:T(2,128)S(1)} %copy.61), channel_id=1, replica_groups=mesh['shard'=128,'tensor'=4] {'shard'}, dimensions={0} | all-to-all | bytes 1048576 | tf_op jit(solution)/shard_map/all_to_all | solution.py:78
  167.5 0.9 copy.62
  168.4 0.0 all-gather.4.cloned.1.call-update
  168.4 0.0 all-gather.6.cloned.1.call-start
  168.5 0.7 all-gather.6.cloned.1.call-update
  169.2 0.0 reduce-scatter.6.cloned.1.call-start
  169.2 0.8 bitcast_convert_fusion.1
  170.0 0.0 reduce-scatter.6.cloned.1.call-update
  170.1 0.6 bitcast_convert_fusion.2
  170.6 30.6 %all-gather.4.cloned.1.call-done = f32[2,512,512]{2,1,0:T(8,128)} async-done(((f32[2,512,128]{2,1,0:T(8,128)}), f32[2,512,512]{2,1,0:T(8,128)}) %all-gather.4.cloned.1.call-update) | async-done | bytes 2097168 | tf_op jit(solution)/shard_map/all_gather | solution.py:79
  201.2 2.0 multiply_reduce_fusion
  203.3 0.1 fusion.8
  203.4 0.0 copy-start.9
  203.4 0.9 copy.73
  204.3 0.5 broadcast_multiply_fusion.1
  204.8 31.3 %all-gather.6.cloned.1.call-done = bf16[2,512,512]{2,1,0:T(8,128)(2,1)} async-done(((bf16[2,128,512]{2,1,0:T(8,128)(2,1)}), bf16[2,512,512]{2,1,0:T(8,128)(2,1)}) %all-gather.6.cloned.1.call-update) | async-done | bytes 1048592 | tf_op jit(solution)/shard_map/all_gather | solution.py:63
  236.1 2.2 multiply_reduce_fusion.2
  238.3 0.0 copy-start.13
  238.3 2.3 multiply_reduce_fusion.3
  240.6 10.0 %all-reduce.1 = (f32[2]{0:T(128)S(1)}, f32[2]{0:T(128)S(1)}, f32[2,32]{1,0:T(2,128)}) all-reduce(f32[2]{0:T(128)S(1)} %get-tuple-element.35, f32[2]{0:T(128)S(1)} %multiply_reduce_fusion.3, f32[2,32]{1,0:T(2,128)} %bitcast_convert_fusion.2), channel_id=1, replica_groups=mesh['shard'=128,'tensor'=4] {'tensor'}, use_global_device_ids=true, to_apply=%region_10.11 | all-reduce | flops 68 | bytes 544 | tf_op jit(solution)/shard_map/psum | solution.py:100
  250.6 0.0 copy-start.15
  250.6 0.1 multiply_bitcast_fusion
  250.7 1.0 copy.65
  251.7 16.6 %all-to-all-start.1 = ((f32[2,512,128]{2,0,1:T(2,128)}), f32[2,512,128]{2,0,1:T(2,128)S(1)}, u32[]{:S(2)}, u32[]{:S(2)}) async-start(f32[2,512,128]{2,0,1:T(2,128)} %copy.65), calls=%async_computation.1 | async-start | bytes 1048576 | tf_op jit(solution)/shard_map/all_to_all | solution.py:103
  268.3 0.7 broadcast_in_dim.48
  269.1 1.3 dynamic-slice
  271.0 0.0 copy-start.2
  271.0 0.0 reduce-scatter.6.cloned.1.call-done
  271.1 1.9 fusion.6
  273.0 13.1 %all_gather.18 = bf16[32,4096]{1,0:T(8,128)(2,1)} all-gather(bf16[32,1024]{1,0:T(8,128)(2,1)S(1)} %get-tuple-element.25), channel_id=1, replica_groups=mesh['shard'=128,'tensor'=4] {'tensor'}, dimensions={1}, use_global_device_ids=true | all-gather | bytes 327680 | tf_op jit(solution)/shard_map/all_gather | solution.py:116
  286.1 1.4 convert_bitcast_fusion
  287.4 7.3 %all-gather = bf16[4,8,2]{1,2,0:T(2,128)(2,1)S(1)} all-gather(bf16[1,8,2]{1,2,0:T(2,128)(2,1)S(1)} %get-tuple-element.21), channel_id=1, replica_groups=mesh['shard'=128,'tensor'=4] {'tensor'}, dimensions={0}, use_global_device_ids=true | all-gather | bytes 160 | tf_op jit(solution)/shard_map/all_gather | solution.py:117
  294.8 0.6 reshape.123
  295.4 4.1 %convolution_add_fusion.1 = f32[2,128,512]{2,1,0:T(8,128)} fusion(f32[2,128,512]{2,1,0:T(8,128)} %param.19, f32[2,512,512]{2,1,0:T(8,128)S(1)} %copy-done.1, s32[]{:T(128)S(6)} %select_n.46), kind=kOutput, calls=%fused_computation.5 | convolution fusion | flops 805437440 | bytes 3670020 | tf_op jit(solution)/shard_map/sqj,sij->sqi/dot_general | solution.py:81
  299.5 2.2 convolution_add_fusion
  301.7 0.4 copy.67
  302.1 0.3 copy.68
  302.5 0.8 gather_fusion.1
  303.3 0.9 fusion.7
  304.2 12.2 %all_gather.17 = bf16[2,8,8,4,512]{4,3,2,1,0:T(4,128)(2,1)S(1)} all-gather(bf16[2,8,8,4,128]{4,3,2,1,0:T(4,128)(2,1)S(1)} %get-tuple-element.29), channel_id=1, replica_groups=mesh['shard'=128,'tensor'=4] {'tensor'}, dimensions={4}, use_global_device_ids=true | all-gather | bytes 655360 | tf_op jit(solution)/shard_map/all_gather | solution.py:115
  316.4 0.8 copy.80
  317.2 0.7 copy.81
  (40 shorter events, 0.2 us)
Async XLA Ops:
  7.2 229.0 %copy-start = (bf16[2,128,512]{2,1,0:T(8,128)(2,1)S(1)}, bf16[2,128,512]{2,1,0:T(8,128)(2,1)}, u32[]{:S(2)}) copy-start(bf16[2,128,512]{2,1,0:T(8,128)(2,1)} %param.22) | copy-start | bytes 786436
  7.2 92.5 %reduce-scatter.8.cloned.1.call-start = ((), (), s32[]{:S(2)}) async-start(), calls=%async_computation.7 | async-start | bytes 1310720
  34.7 29.4 %copy-start.16 = (s32[128]{0:T(128)S(1)}, s32[128]{0:T(128)}, u32[]{:S(2)}) copy-start(s32[128]{0:T(128)} %param.25) | copy-start | bytes 1540
  64.1 137.2 %all-gather.4.cloned.1.call-start = ((), (), s32[]{:S(2)}) async-start(), calls=%async_computation.4 | async-start | bytes 2621440 | tf_op jit(solution)/shard_map/all_gather | solution.py:79
  64.8 0.5 copy-start.12
  118.7 50.5 %copy-start.5 = (bf16[1,32,4096]{2,1,0:T(8,128)(2,1)S(1)}, bf16[1,32,4096]{2,1,0:T(8,128)(2,1)}, u32[]{:S(2)}) copy-start(bf16[1,32,4096]{2,1,0:T(8,128)(2,1)} %param.26) | copy-start | bytes 786436
  118.9 51.1 %copy-start.17 = (bf16[1,2,32]{2,1,0:T(2,128)(2,1)S(1)}, bf16[1,2,32]{2,1,0:T(2,128)(2,1)}, u32[]{:S(2)}) copy-start(bf16[1,2,32]{2,1,0:T(2,128)(2,1)} %param.30) | copy-start | bytes 388
  168.4 34.9 %copy-start.10 = (f32[2,512]{1,0:T(2,128)S(1)}, f32[2,512]{1,0:T(2,128)}, u32[]{:S(2)}) copy-start(f32[2,512]{1,0:T(2,128)} %param.23) | copy-start | bytes 12292
  168.4 34.9 %copy-start.11 = (f32[2,512]{1,0:T(2,128)S(1)}, f32[2,512]{1,0:T(2,128)}, u32[]{:S(2)}) copy-start(f32[2,512]{1,0:T(2,128)} %param.24) | copy-start | bytes 12292
  168.4 67.7 %all-gather.6.cloned.1.call-start = ((), (), s32[]{:S(2)}) async-start(), calls=%async_computation.5 | async-start | bytes 1310720 | tf_op jit(solution)/shard_map/all_gather | solution.py:63
  169.2 101.9 %reduce-scatter.6.cloned.1.call-start = ((), (), s32[]{:S(2)}) async-start(), calls=%async_computation.6 | async-start | bytes 655360 | tf_op jit(solution)/shard_map/reduce_scatter | solution.py:69
  201.2 34.9 %copy-start.1 = (f32[2,512,512]{2,1,0:T(8,128)S(1)}, f32[2,512,512]{2,1,0:T(8,128)}, u32[]{:S(2)}) copy-start(f32[2,512,512]{2,1,0:T(8,128)} %all-gather.4.cloned.1.call-done) | copy-start | bytes 6291460
  203.4 34.9 %copy-start.8 = (f32[2,512]{1,0:T(2,128)}, f32[2,512]{1,0:T(2,128)S(1)}, u32[]{:S(2)}) copy-start(f32[2,512]{1,0:T(2,128)S(1)} %get-tuple-element.56) | copy-start | bytes 12292
  203.4 34.9 %copy-start.9 = (f32[2,512]{1,0:T(2,128)}, f32[2,512]{1,0:T(2,128)S(1)}, u32[]{:S(2)}) copy-start(f32[2,512]{1,0:T(2,128)S(1)} %get-tuple-element.57) | copy-start | bytes 12292
  238.3 32.8 %copy-start.7 = (f32[32,1024]{1,0:T(8,128)S(1)}, f32[32,1024]{1,0:T(8,128)}, u32[]{:S(2)}) copy-start(f32[32,1024]{1,0:T(8,128)} %param.27) | copy-start | bytes 393220
  238.3 32.7 %copy-start.13 = (s32[128]{0:T(128)S(1)}, s32[128]{0:T(128)}, u32[]{:S(2)}) copy-start(s32[128]{0:T(128)} %copy-done.12) | copy-start | bytes 1540
  250.6 35.5 %copy-start.14 = (f32[2,8]{1,0:T(2,128)S(1)}, f32[2,8]{1,0:T(2,128)}, u32[]{:S(2)}) copy-start(f32[2,8]{1,0:T(2,128)} %param.31) | copy-start | bytes 196
  250.6 35.5 %copy-start.15 = (f32[2,8]{1,0:T(2,128)S(1)}, f32[2,8]{1,0:T(2,128)}, u32[]{:S(2)}) copy-start(f32[2,8]{1,0:T(2,128)} %param.32) | copy-start | bytes 196
  251.7 50.0 %all-to-all-start.1 = ((f32[2,512,128]{2,0,1:T(2,128)}), f32[2,512,128]{2,0,1:T(2,128)S(1)}, u32[]{:S(2)}, u32[]{:S(2)}) async-start(f32[2,512,128]{2,0,1:T(2,128)} %copy.65), calls=%async_computation.1 | async-start | bytes 1048576 | tf_op jit(solution)/shard_map/all_to_all | solution.py:103
  271.0 28.5 %copy-start.2 = (f32[1,2,128,4,128]{4,3,2,1,0:T(4,128)S(1)}, f32[1,2,128,4,128]{4,3,2,1,0:T(4,128)}, u32[]{:S(2)}) copy-start(f32[1,2,128,4,128]{4,3,2,1,0:T(4,128)} %copy.62) | copy-start | bytes 1572868
  295.4 4.1 %copy-start.4 = (f32[2,128,512]{2,1,0:T(8,128)S(1)}, f32[2,128,512]{2,1,0:T(8,128)}, u32[]{:S(2)}) copy-start(f32[2,128,512]{2,1,0:T(8,128)} %param.20) | copy-start | bytes 1572868
  301.7 1.6 copy-start.6
  302.1 15.1 %copy-start.3 = (bf16[32,4096]{1,0:T(8,128)(2,1)S(1)}, bf16[32,4096]{1,0:T(8,128)(2,1)}, u32[]{:S(2)}) copy-start(bf16[32,4096]{1,0:T(8,128)(2,1)} %all_gather.18) | copy-start | bytes 786436
Sparse Core Ops, SparseCore 0:
  64.2 35.4 reduce-scatter.7
  168.5 32.6 all-gather.3
  203.3 32.7 all-gather.5
  239.4 29.7 reduce-scatter.5
where the time goes:
time: 325 us; the launch traced here: 324 us
  waiting for transfers between devices  96.6 us (30%)
  blocking collectives  91.1 us (28%)
  local copies, waits for them, and re-layouts  83.5 us (26%)
  starting transfers between devices  16.8 us (5%)
  between operations  14.8 us (5%)
  other arithmetic  13.3 us (4%)
  matrix products  8.48 us (3%)
    unnamed x44, local copies, waits for them, and re-layouts  76.9 us
    all_to_all x1, blocking collectives, per_device(): lax.all_to_all(outgoing, 'shard', split_axis=0, concat_axis=2, tiled=True)  48.5 us
    unnamed x5, waiting for transfers between devices  34.7 us
    all_gather x1, waiting for transfers between devices, per_device(): left_full = lax.all_gather(left_roots, 'tensor', axis=1, tiled=True)  31.3 us
    all_gather x1, waiting for transfers between devices, per_device(): full_block = lax.all_gather(own_cols, 'tensor', axis=2, tiled=True)  30.6 us
    all_to_all x1, starting transfers between devices, per_device(): lax.all_to_all(update, 'shard', split_axis=1, concat_axis=0, tiled=True)  16.6 us
    all_gather x1, blocking collectives, per_device(): lax.all_gather(emb_low, 'tensor', axis=1, tiled=True)  13.1 us
    all_gather x1, blocking collectives, per_device(): lax.all_gather(wo_new.astype(jnp.bfloat16), 'tensor', axis=4, tiled=True)  12.2 us
  transfers between devices with their start and end apart: 5, of which 3 were waited for; matrix products, arithmetic and copies ran while one was open for 7% of the time, Pallas kernels for 0%

commit v1 on v0

v1 whole, which is shorter than its diff:
```python
import functools

import jax
import jax.numpy as jnp
from jax import lax
from jax.experimental import pallas as pl
from jax.experimental.pallas import tpu as pltpu
from jax.sharding import PartitionSpec as P


beta_one = 0.9
beta_two = 0.95
bias_one = 1.0 - 0.9**10
bias_two = 1.0 - 0.95**10
adam_eps = 1e-08
learn_rate = 0.01
decay_rate = 0.1
graft_eps = 1e-06
factor_eps = 1e-08
low = jnp.bfloat16
full = jnp.float32


def adamw_step(gradient, master, first_moment, second_moment):
    mean_new = beta_one * first_moment + (1.0 - beta_one) * gradient
    var_new = beta_two * second_moment + (1.0 - beta_two) * gradient * gradient
    adam_dir = mean_new / bias_one / (jnp.sqrt(var_new / bias_two) + adam_eps)
    master_new = master - learn_rate * (adam_dir + decay_rate * master)
    return (master_new, mean_new, var_new, master_new.astype(low))


def split_kernel(grads, parts):
    lanes = parts.shape[3]
    for member in range(parts.shape[0]):
        parts[member] = grads[:, :, member * lanes : (member + 1) * lanes]


def split_columns(grads, ways):
    blocks, rows, columns = grads.shape
    vmem = pl.BlockSpec(memory_space=pltpu.VMEM)
    return pl.pallas_call(
        split_kernel,
        out_shape=jax.ShapeDtypeStruct((ways, blocks, rows, columns // ways), grads.dtype),
        in_specs=[vmem],
        out_specs=vmem,
        name="split_columns",
    )(grads)


def place_kernel(slot_of, terms, slots):
    slots[...] = jnp.zeros_like(slots)
    micro_count, block_count = terms.shape[:2]

    def place(block, carry):
        total = terms[0, block].astype(full)
        for micro in range(1, micro_count):
            total = total + terms[micro, block].astype(full)
        slots[slot_of[block]] = (total / micro_count).astype(low)
        return carry

    lax.fori_loop(0, block_count, place, 0, unroll=8)


def place_blocks(slot_of, terms, slot_total):
    vmem = pl.BlockSpec(memory_space=pltpu.VMEM)
    return pl.pallas_call(
        place_kernel,
        out_shape=jax.ShapeDtypeStruct((slot_total,) + terms.shape[2:], low),
        in_specs=[pl.BlockSpec(memory_space=pltpu.SMEM), vmem],
        out_specs=vmem,
        name="place_blocks",
    )(slot_of, terms)


def core_kernel(here, columns, own, *rest, slot_count):
    ways = columns.shape[0]
    others, (row_old, col_old, update, row_new, col_new) = rest[: ways - 1], rest[ways - 1 :]
    factors = (own,) + tuple(others)
    quarter = own.shape[2]
    for slot in range(slot_count):
        block = jnp.concatenate([columns[member, slot] for member in range(ways)], axis=1)
        left = jnp.concatenate([factor[0, slot] for factor in factors], axis=0)
        right = jnp.concatenate([factor[1, slot] for factor in factors], axis=0)
        half = lax.dot_general(
            block, right, (((1,), (1,)), ((), ())), preferred_element_type=full
        ).astype(low)
        shampoo = jnp.dot(left, half, preferred_element_type=full)
        wide = block.astype(full)
        squares = wide * wide
        rows = beta_two * row_old[:, slot : slot + 1] + (1.0 - beta_two) * jnp.mean(
            squares, axis=1, keepdims=True
        )
        cols = beta_two * col_old[slot : slot + 1, :] + (1.0 - beta_two) * jnp.mean(
            squares, axis=0, keepdims=True
        )
        row_new[:, slot : slot + 1] = rows
        col_new[slot : slot + 1, :] = cols
        level = jnp.mean(rows, axis=0, keepdims=True)
        adam_dir = wide / (jnp.sqrt(rows) * jnp.sqrt(cols / level) + factor_eps)
        adam_total = jnp.sum(
            jnp.sum(adam_dir * adam_dir, axis=0, keepdims=True), axis=1, keepdims=True
        )
        shampoo_total = jnp.sum(
            jnp.sum(shampoo * shampoo, axis=0, keepdims=True), axis=1, keepdims=True
        )
        ratio = jnp.sqrt(adam_total) / (jnp.sqrt(shampoo_total) + graft_eps)
        for k in range(ways):
            member = lax.rem(here[0] - k + ways, ways)
            update[slot, pl.ds(member * quarter, quarter), :] = (
                shampoo[k * quarter : (k + 1) * quarter, :quarter] * ratio
            ).astype(low)


def precondition(here, columns, factors, row_old, col_old):
    _, slot_count, side, quarter = columns.shape
    vmem = pl.BlockSpec(memory_space=pltpu.VMEM)
    return pl.pallas_call(
        functools.partial(core_kernel, slot_count=slot_count),
        out_shape=(
            jax.ShapeDtypeStruct((slot_count, side, quarter), low),
            jax.ShapeDtypeStruct((side, slot_count), full),
            jax.ShapeDtypeStruct((slot_count, side), full),
        ),
        in_specs=[pl.BlockSpec(memory_space=pltpu.SMEM)] + [vmem] * (3 + len(factors)),
        out_specs=(vmem, vmem, vmem),
        name="precondition",
    )(here, columns, *factors, row_old, col_old)


def apply_kernel(slot_of, updates, master, master_new, weights):
    def step(block, carry):
        update = updates[slot_of[block]].astype(full)
        old = master[block]
        new = old - learn_rate * (update + decay_rate * old)
        master_new[block] = new
        rounded = new.astype(low)
        for copy in range(weights.shape[0]):
            weights[copy, block] = rounded
        return carry

    lax.fori_loop(0, master.shape[0], step, 0, unroll=8)


def apply_updates(slot_of, updates, master, copies):
    vmem = pl.BlockSpec(memory_space=pltpu.VMEM)
    return pl.pallas_call(
        apply_kernel,
        out_shape=(
            jax.ShapeDtypeStruct(master.shape, full),
            jax.ShapeDtypeStruct((copies,) + master.shape, low),
        ),
        in_specs=[pl.BlockSpec(memory_space=pltpu.SMEM), vmem, vmem],
        out_specs=(vmem, vmem),
        name="apply_updates",
    )(slot_of, updates, master)


def slots_of(owners, slot_count):
    ids = jnp.arange(owners.shape[0], dtype=jnp.int32)
    earlier = (owners[:, None] == owners[None, :]) & (ids[None, :] < ids[:, None])
    return owners * slot_count + jnp.sum(earlier.astype(jnp.int32), axis=1)


def in_order(pieces, position):
    count = len(pieces)
    turned = [pieces[(-j) % count] for j in range(count)]
    return lax.dynamic_slice_in_dim(
        jnp.stack(turned + turned), (count - position) % count, count, 0
    )


def from_peers(value_for, axis):
    count = lax.axis_size(axis)
    pieces = [value_for(0)]
    for k in range(1, count):
        value = value_for(k)
        pieces.append(lax.ppermute(value, axis, [(i, (i + k) % count) for i in range(count)]))
    return pieces


def per_device(
    wo_grads,
    wo_master,
    left_stats,
    right_stats,
    left_roots,
    right_roots,
    row_moments,
    col_moments,
    owners,
    emb_grads,
    emb_master,
    emb_mean,
    emb_var,
    gain_grads,
    gain_master,
    gain_mean,
    gain_var,
):
    ways = lax.axis_size("tensor")
    owner_count = lax.axis_size("shard")
    here = lax.axis_index("tensor")
    slot_count, quarter, side = left_stats.shape
    rows_dev = wo_master.shape[3]
    block_count = wo_master.shape[0] * wo_master.shape[1] * wo_master.shape[2]

    slot_of = slots_of(owners, slot_count)
    wo_parts = split_columns(wo_grads.reshape(block_count, rows_dev, side), ways)
    wo_terms = lax.all_to_all(wo_parts, "tensor", 0, 0, tiled=True)

    emb_rows, emb_cols = emb_master.shape
    gain_rows, gain_cols = gain_master.shape
    pad_rows = 8
    emb_parts = emb_grads[0].reshape(emb_rows, ways, emb_cols).transpose(1, 0, 2)
    gain_parts = gain_grads[0].reshape(gain_rows, ways, gain_cols).transpose(1, 0, 2)
    gain_parts = jnp.pad(
        gain_parts, ((0, 0), (0, pad_rows - gain_rows), (0, emb_cols - gain_cols))
    )
    small_parts = jnp.concatenate([emb_parts, gain_parts], axis=1)
    small_pieces = from_peers(
        lambda k: lax.dynamic_index_in_dim(small_parts, (here + k) % ways, 0, keepdims=False),
        "tensor",
    )
    small_sum = sum(piece.astype(full) for piece in small_pieces)

    outgoing = place_blocks(slot_of, wo_terms, owner_count * slot_count)
    outgoing = outgoing.reshape(owner_count, slot_count, rows_dev, quarter)
    own_cols = lax.all_to_all(outgoing, "shard", 0, 0, tiled=True)
    roots = jnp.stack([left_roots, right_roots])
    factors = from_peers(lambda k: roots, "tensor")

    own_cols, factors = lax.optimization_barrier((own_cols, factors))
    own_cols = own_cols.transpose(1, 0, 2, 3).reshape(slot_count, side, quarter)
    gathered = lax.all_to_all(
        jnp.broadcast_to(own_cols[None], (ways,) + own_cols.shape), "tensor", 0, 0, tiled=True
    )
    update, row_new, col_new = precondition(
        here.reshape(1).astype(jnp.int32), gathered, factors, row_moments.T, col_moments
    )
    row_new = row_new.T
    update = update.reshape(slot_count, owner_count, rows_dev, quarter).transpose(1, 0, 2, 3)
    returned = lax.all_to_all(update, "shard", 0, 0, tiled=True)

    block = gathered.transpose(1, 2, 0, 3).reshape(slot_count, side, side)
    own_rows = lax.dynamic_slice_in_dim(block, here * quarter, quarter, 1)
    left_new = left_stats + jnp.einsum("sqj,sij->sqi", own_rows, block, preferred_element_type=full)
    right_new = right_stats + jnp.einsum(
        "siq,sij->sqj", own_cols, block, preferred_element_type=full
    )

    small_grad = small_sum / ways
    emb_new, emb_mean_new, emb_var_new, emb_low = adamw_step(
        small_grad[:emb_rows], emb_master, emb_mean, emb_var
    )
    gain_new, gain_mean_new, gain_var_new, gain_low = adamw_step(
        small_grad[emb_rows : emb_rows + gain_rows, :gain_cols], gain_master, gain_mean, gain_var
    )
    gain_low = jnp.pad(gain_low, ((0, pad_rows - gain_rows), (0, emb_cols - gain_cols)))
    small_low = jnp.concatenate([emb_low, gain_low], axis=0)
    small_all = in_order(from_peers(lambda k: small_low, "tensor"), here)
    emb_weights = small_all[:, :emb_rows].transpose(1, 0, 2).reshape(emb_rows, ways * emb_cols)
    gain_weights = small_all[:, emb_rows : emb_rows + gain_rows, :gain_cols]
    gain_weights = gain_weights.transpose(1, 0, 2).reshape(gain_rows, ways * gain_cols)

    wo_new, wo_low = apply_updates(
        slot_of,
        returned.reshape(owner_count * slot_count, rows_dev, quarter),
        wo_master.reshape(block_count, rows_dev, quarter),
        ways,
    )
    wo_low = lax.all_to_all(wo_low, "tensor", 0, 0, tiled=True)
    wo_weights = wo_low.transpose(1, 2, 0, 3).reshape(wo_master.shape[:3] + (rows_dev, side))
    return (
        wo_new.reshape(wo_master.shape),
        wo_weights,
        left_new,
        right_new,
        row_new,
        col_new,
        emb_new,
        emb_mean_new,
        emb_var_new,
        emb_weights,
        gain_new,
        gain_mean_new,
        gain_var_new,
        gain_weights,
    )


def solution(mesh):
    in_specs = (
        P("tensor", None, None, None, "shard", None),
        P(None, None, None, "shard", "tensor"),
        P("shard", "tensor", None),
        P("shard", "tensor", None),
        P("shard", "tensor", None),
        P("shard", "tensor", None),
        P("shard", None),
        P("shard", None),
        P(),
        P("tensor", "shard", None),
        P("shard", "tensor"),
        P("shard", "tensor"),
        P("shard", "tensor"),
        P("tensor", None, "shard"),
        P(None, ("shard", "tensor")),
        P(None, ("shard", "tensor")),
        P(None, ("shard", "tensor")),
    )
    out_specs = (
        P(None, None, None, "shard", "tensor"),
        P(None, None, None, "shard", None),
        P("shard", "tensor", None),
        P("shard", "tensor", None),
        P("shard", None),
        P("shard", None),
        P("shard", "tensor"),
        P("shard", "tensor"),
        P("shard", "tensor"),
        P("shard", None),
        P(None, ("shard", "tensor")),
        P(None, ("shard", "tensor")),
        P(None, ("shard", "tensor")),
        P(None, "shard"),
    )

    return jax.shard_map(per_device, mesh=mesh, in_specs=in_specs, out_specs=out_specs, check_vma=False)
```

time: 325 us -> 168 us (0.52)
  the two profiles are of different devices: /device:TPU:40 before, /device:TPU:32 now
where the time goes in v1:
time: 168 us; the launch traced here: 167 us
  starting transfers between devices  79.7 us (47%)
  waiting for transfers between devices  56.3 us (34%)
  local copies, waits for them, and re-layouts  13.3 us (8%)
  Pallas kernels  11 us (7%)
  other arithmetic  3.62 us (2%)
  matrix products  2.42 us (1%)
    ppermute x9, starting transfers between devices, from_peers(): lax.ppermute(value, axis, [(i, (i + k) % count) for i in range(count)])  31 us
    all_to_all x1, waiting for transfers between devices, per_device(): returned = lax.all_to_all(update, 'shard', 0, 0, tiled=True)  20.5 us
    ppermute x9, waiting for transfers between devices, from_peers(): lax.ppermute(value, axis, [(i, (i + k) % count) for i in range(count)])  20.3 us
    all_to_all x1, starting transfers between devices, per_device(): own_cols = lax.all_to_all(outgoing, 'shard', 0, 0, tiled=True)  19.3 us
    all_to_all x1, starting transfers between devices, per_device(): returned = lax.all_to_all(update, 'shard', 0, 0, tiled=True)  16.1 us
    all_to_all x1, waiting for transfers between devices, per_device(): wo_terms = lax.all_to_all(wo_parts, 'tensor', 0, 0, tiled=True)  8.77 us
    unnamed x59, local copies, waits for them, and re-layouts  8.21 us
    all_to_all x1, waiting for transfers between devices, per_device(): wo_low = lax.all_to_all(wo_low, 'tensor', 0, 0, tiled=True)  6.69 us
  transfers between devices with their start and end apart: 14, of which 8 were waited for; matrix products, arithmetic and copies ran while one was open for 7% of the time, Pallas kernels for 3%

profile of v1, /device:TPU:32, one launch (start us, length us, event | category | flops | bytes accessed | tf_op | source)
XLA Modules:
  0.0 167.5 jit_solution(9682986702992646932)
XLA Ops:
  0.6 2.0 %split_columns.1 = bf16[4,128,4,128]{3,2,1,0:T(4,128)(2,1)} custom-call(bf16[128,4,512]{2,1,0:T(4,128)(2,1)} %bitcast.70), custom_call_target="tpu_custom_call" | custom-call | tf_op jit(solution)/shard_map/split_columns/pallas_call | solution.py:41
  2.7 4.4 %all-to-all-start = ((bf16[4,128,4,128]{3,2,1,0:T(4,128)(2,1)}), bf16[4,128,4,128]{3,2,1,0:T(4,128)(2,1)S(1)}, u32[]{:S(2)}, u32[]{:S(2)}) async-start(bf16[4,128,4,128]{3,2,1,0:T(4,128)(2,1)} %split_columns.1), calls=%async_computation | async-start | bytes 1048576 | tf_op jit(solution)/shard_map/all_to_all | solution.py:209
  7.1 0.2 convert_reduce_fusion
  7.3 0.5 multiply_add_fusion.2.slot_of
  7.8 8.8 %all-to-all-done.terms = bf16[4,128,4,128]{3,2,1,0:T(4,128)(2,1)S(1)} async-done(((bf16[4,128,4,128]{3,2,1,0:T(4,128)(2,1)}), bf16[4,128,4,128]{3,2,1,0:T(4,128)(2,1)S(1)}, u32[]{:S(2)}, u32[]{:S(2)}) %all-to-all-start) | async-done | bytes 524320 | tf_op jit(solution)/shard_map/all_to_all | solution.py:209
  16.6 0.8 copy-done.2
  17.4 2.1 %place_blocks.1 = bf16[256,4,128]{2,1,0:T(4,128)(2,1)} custom-call(s32[128]{0:T(128)} %multiply_add_fusion.2.slot_of, bf16[4,128,4,128]{3,2,1,0:T(4,128)(2,1)} %copy-done.2), custom_call_target="tpu_custom_call" | custom-call | tf_op jit(solution)/shard_map/place_blocks/pallas_call | solution.py:66
  19.4 19.3 %all-to-all-start.1 = ((bf16[128,2,4,128]{3,2,1,0:T(4,128)(2,1)}), bf16[128,2,4,128]{3,2,1,0:T(4,128)(2,1)S(1)}, u32[]{:S(2)}, u32[]{:S(2)}) async-start(bf16[128,2,4,128]{3,2,1,0:T(4,128)(2,1)} %bitcast.69), calls=%async_computation.1 | async-start | bytes 524288 | tf_op jit(solution)/shard_map/all_to_all | solution.py:228
  38.8 0.0 copy-start.21
  38.8 0.6 copy-done.21
  39.5 0.1 reshape_squeeze.7
  39.5 0.2 reshape_squeeze.6
  39.8 0.1 fusion.1
  39.9 0.6 constant_dynamic-slice_fusion.2
  40.5 0.0 copy-start.13
  40.6 0.0 copy-start.12
  40.6 3.2 %collective-permute-start.5 = (bf16[40,1024]{1,0:T(8,128)(2,1)S(1)}, bf16[40,1024]{1,0:T(8,128)(2,1)S(1)}, u32[]{:S(2)}, u32[]{:S(2)}) collective-permute-start(bf16[40,1024]{1,0:T(8,128)(2,1)S(1)} %bitcast.79), channel_id=1, source_target_pairs={{0,3},{1,0},{2,1},{3,2},{4,7},{5,4},{6,5},{7,6},{8,11},{9,8},{10,9... | collective-permute-start | bytes 245768 | tf_op jit(solution)/shard_map/ppermute | solution.py:177
  43.9 3.4 %collective-permute-start.4 = (bf16[40,1024]{1,0:T(8,128)(2,1)S(1)}, bf16[40,1024]{1,0:T(8,128)(2,1)S(1)}, u32[]{:S(2)}, u32[]{:S(2)}) collective-permute-start(bf16[40,1024]{1,0:T(8,128)(2,1)S(1)} %bitcast.77), channel_id=1, source_target_pairs={{0,2},{1,3},{2,0},{3,1},{4,6},{5,7},{6,4},{7,5},{8,10},{9,11},{10,... | collective-permute-start | bytes 245768 | tf_op jit(solution)/shard_map/ppermute | solution.py:177
  47.3 1.9 %collective-permute-start.3 = (bf16[40,1024]{1,0:T(8,128)(2,1)S(1)}, bf16[40,1024]{1,0:T(8,128)(2,1)S(1)}, u32[]{:S(2)}, u32[]{:S(2)}) collective-permute-start(bf16[40,1024]{1,0:T(8,128)(2,1)S(1)} %bitcast.78), channel_id=1, source_target_pairs={{0,1},{1,2},{2,3},{3,0},{4,5},{5,6},{6,7},{7,4},{8,9},{9,10},{10,1... | collective-permute-start | bytes 245768 | tf_op jit(solution)/shard_map/ppermute | solution.py:177
  49.2 0.1 pad_maximum_fusion.own
  49.3 0.0 copy-start.3
  49.3 3.9 %collective-permute-start = (bf16[2,2,128,512]{3,2,1,0:T(8,128)(2,1)S(1)}, bf16[2,2,128,512]{3,2,1,0:T(8,128)(2,1)S(1)}, u32[]{:S(2)}, u32[]{:S(2)}) collective-permute-start(bf16[2,2,128,512]{3,2,1,0:T(8,128)(2,1)S(1)} %pad_maximum_fusion.own), channel_id=1, source_target_pairs={{0,1},{1,2},{2,3},{3,0},{4,5},{5,6},{6,7},{7,4},{8,9},{9,10},{10,1... | collective-permute-start | bytes 1572872 | tf_op jit(solution)/shard_map/ppermute | solution.py:177
  53.2 4.6 %collective-permute-start.1 = (bf16[2,2,128,512]{3,2,1,0:T(8,128)(2,1)S(1)}, bf16[2,2,128,512]{3,2,1,0:T(8,128)(2,1)S(1)}, u32[]{:S(2)}, u32[]{:S(2)}) collective-permute-start(bf16[2,2,128,512]{3,2,1,0:T(8,128)(2,1)S(1)} %pad_maximum_fusion.own), channel_id=1, source_target_pairs={{0,2},{1,3},{2,0},{3,1},{4,6},{5,7},{6,4},{7,5},{8,10},{9,11},{10,... | collective-permute-start | bytes 1572872 | tf_op jit(solution)/shard_map/ppermute | solution.py:177
  57.8 3.4 %collective-permute-start.2 = (bf16[2,2,128,512]{3,2,1,0:T(8,128)(2,1)S(1)}, bf16[2,2,128,512]{3,2,1,0:T(8,128)(2,1)S(1)}, u32[]{:S(2)}, u32[]{:S(2)}) collective-permute-start(bf16[2,2,128,512]{3,2,1,0:T(8,128)(2,1)S(1)} %pad_maximum_fusion.own), channel_id=1, source_target_pairs={{0,3},{1,0},{2,1},{3,2},{4,7},{5,4},{6,5},{7,6},{8,11},{9,8},{10,9... | collective-permute-start | bytes 1572872 | tf_op jit(solution)/shard_map/ppermute | solution.py:177
  61.2 0.0 copy-start.17
  61.2 0.7 copy-done.17
  61.9 0.9 copy.78
  62.8 0.0 copy-start.16
  62.8 0.1 fusion.5
  62.9 0.8 copy-done.14
  63.7 0.1 copy-done.15
  63.7 0.1 copy-done.16
  63.8 0.8 fusion.12
  64.6 2.2 %collective-permute-done.rest_0_ = bf16[2,2,128,512]{3,2,1,0:T(8,128)(2,1)S(1)} collective-permute-done((bf16[2,2,128,512]{3,2,1,0:T(8,128)(2,1)S(1)}, bf16[2,2,128,512]{3,2,1,0:T(8,128)(2,1)S(1)}, u32[]{:S(2)}, u32[]{:S(2)}) %collective-permute-start) | collective-permute-done | bytes 524320 | tf_op jit(solution)/shard_map/ppermute | solution.py:177
  66.9 11.3 %collective-permute-done.1.rest_1_ = bf16[2,2,128,512]{3,2,1,0:T(8,128)(2,1)S(1)} collective-permute-done((bf16[2,2,128,512]{3,2,1,0:T(8,128)(2,1)S(1)}, bf16[2,2,128,512]{3,2,1,0:T(8,128)(2,1)S(1)}, u32[]{:S(2)}, u32[]{:S(2)}) %collective-permute-start.1) | collective-permute-done | bytes 524320 | tf_op jit(solution)/shard_map/ppermute | solution.py:177
  78.2 1.4 collective-permute-done.2.rest_2_
  79.6 0.1 copy.77
  79.7 1.1 broadcast_in_dim.5
  80.8 0.0 copy-start.19
  80.8 4.6 %all-to-all-start.2 = ((bf16[4,2,512,128]{3,2,1,0:T(8,128)(2,1)}), bf16[4,2,512,128]{3,2,1,0:T(8,128)(2,1)S(1)}, u32[]{:S(2)}, u32[]{:S(2)}) async-start(bf16[4,2,512,128]{3,2,1,0:T(8,128)(2,1)} %broadcast_in_dim.5), calls=%async_computation.2 | async-start | bytes 2097152 | tf_op jit(solution)/shard_map/all_to_all | solution.py:234
  85.5 0.6 fusion.14
  86.1 0.6 fusion.8
  86.7 5.1 %collective-permute-start.6 = (bf16[40,1024]{1,0:T(8,128)(2,1)}, bf16[40,1024]{1,0:T(8,128)(2,1)S(1)}, u32[]{:S(2)}, u32[]{:S(2)}) collective-permute-start(bf16[40,1024]{1,0:T(8,128)(2,1)} %fusion.8), channel_id=1, source_target_pairs={{0,3},{1,0},{2,1},{3,2},{4,7},{5,4},{6,5},{7,6},{8,11},{9,8},{10,9... | collective-permute-start | bytes 245768 | tf_op jit(solution)/shard_map/ppermute | solution.py:177
  91.8 2.8 %collective-permute-start.7 = (bf16[40,1024]{1,0:T(8,128)(2,1)}, bf16[40,1024]{1,0:T(8,128)(2,1)S(1)}, u32[]{:S(2)}, u32[]{:S(2)}) collective-permute-start(bf16[40,1024]{1,0:T(8,128)(2,1)} %fusion.8), channel_id=1, source_target_pairs={{0,2},{1,3},{2,0},{3,1},{4,6},{5,7},{6,4},{7,5},{8,10},{9,11},{10,... | collective-permute-start | bytes 245768 | tf_op jit(solution)/shard_map/ppermute | solution.py:177
  94.6 2.8 %collective-permute-start.8 = (bf16[40,1024]{1,0:T(8,128)(2,1)}, bf16[40,1024]{1,0:T(8,128)(2,1)S(1)}, u32[]{:S(2)}, u32[]{:S(2)}) collective-permute-start(bf16[40,1024]{1,0:T(8,128)(2,1)} %fusion.8), channel_id=1, source_target_pairs={{0,1},{1,2},{2,3},{3,0},{4,5},{5,6},{6,7},{7,4},{8,9},{9,10},{10,1... | collective-permute-start | bytes 245768 | tf_op jit(solution)/shard_map/ppermute | solution.py:177
  97.4 4.6 %collective-permute-done.6 = bf16[40,1024]{1,0:T(8,128)(2,1)S(1)} collective-permute-done((bf16[40,1024]{1,0:T(8,128)(2,1)}, bf16[40,1024]{1,0:T(8,128)(2,1)S(1)}, u32[]{:S(2)}, u32[]{:S(2)}) %collective-permute-start.6) | collective-permute-done | bytes 81952 | tf_op jit(solution)/shard_map/ppermute | solution.py:177
  102.0 0.7 collective-permute-done.7
  102.8 1.0 copy-done
  103.8 4.7 %precondition.1 = (bf16[2,512,128]{2,1,0:T(8,128)(2,1)}, f32[512,2]{1,0:T(8,128)}, f32[2,512]{1,0:T(2,128)}) custom-call(s32[1]{0:T(128)} %bitcast.here, bf16[4,2,512,128]{3,2,1,0:T(8,128)(2,1)} %copy-done, bf16[2,2,128,512]{3,2,1,0:T(8,128)(2,1)} %copy-done.3, bf16[2,2,128,512]{3,2,1,0:T(8,128)(2,1)} %copy-done.7, bf16[2,2,128,512]{3,2,1,0:T(8,128)(2,1)} %copy-done.8, ...), custom_call_target="tpu_custom_call" | custom-call | tf_op jit(solution)/shard_map/precondition/pallas_call | solution.py:117
  108.4 1.7 %copy.106 = bf16[2,128,4,128]{3,2,0,1:T(4,128)(2,1)} copy(bf16[2,128,4,128]{3,2,1,0:T(4,128)(2,1)} %bitcast.74) | data formatting | bytes 524288 | tf_op jit(solution)/shard_map/reshape | solution.py:241
  110.2 16.1 %all-to-all-start.3 = ((bf16[128,2,4,128]{3,2,1,0:T(4,128)(2,1)}), bf16[128,2,4,128]{3,2,1,0:T(4,128)(2,1)S(1)}, u32[]{:S(2)}, u32[]{:S(2)}) async-start(bf16[128,2,4,128]{3,2,1,0:T(4,128)(2,1)} %bitcast.55), calls=%async_computation.3 | async-start | bytes 524288 | tf_op jit(solution)/shard_map/all_to_all | solution.py:242
  126.4 0.7 copy.100
  127.2 0.6 reshape.77
  127.8 0.5 copy.81
  128.3 20.5 %all-to-all-done.3 = bf16[128,2,4,128]{3,2,1,0:T(4,128)(2,1)S(1)} async-done(((bf16[128,2,4,128]{3,2,1,0:T(4,128)(2,1)}), bf16[128,2,4,128]{3,2,1,0:T(4,128)(2,1)S(1)}, u32[]{:S(2)}, u32[]{:S(2)}) %all-to-all-start.3) | async-done | bytes 262176 | tf_op jit(solution)/shard_map/all_to_all | solution.py:242
  148.8 0.7 copy-done.4
  149.5 2.3 %apply_updates.1 = (f32[128,4,128]{2,1,0:T(4,128)}, bf16[4,128,4,128]{3,2,1,0:T(4,128)(2,1)}) custom-call(s32[128]{0:T(128)} %multiply_add_fusion.2.slot_of, bf16[256,4,128]{2,1,0:T(4,128)(2,1)} %bitcast.66, f32[128,4,128]{2,1,0:T(4,128)} %bitcast.71), custom_call_target="tpu_custom_call" | custom-call | tf_op jit(solution)/shard_map/apply_updates/pallas_call | solution.py:146
  151.8 4.2 %all-to-all-start.4 = ((bf16[4,128,4,128]{3,2,1,0:T(4,128)(2,1)}), bf16[4,128,4,128]{3,2,1,0:T(4,128)(2,1)S(1)}, u32[]{:S(2)}, u32[]{:S(2)}) async-start(bf16[4,128,4,128]{3,2,1,0:T(4,128)(2,1)} %get-tuple-element.31), calls=%async_computation.4 | async-start | bytes 1048576 | tf_op jit(solution)/shard_map/all_to_all | solution.py:271
  156.0 1.1 convolution_add_fusion.1
  157.1 0.7 copy.89
  157.8 1.3 convolution_add_fusion
  159.1 6.7 %all-to-all-done.4 = bf16[4,128,4,128]{3,2,1,0:T(4,128)(2,1)S(1)} async-done(((bf16[4,128,4,128]{3,2,1,0:T(4,128)(2,1)}), bf16[4,128,4,128]{3,2,1,0:T(4,128)(2,1)S(1)}, u32[]{:S(2)}, u32[]{:S(2)}) %all-to-all-start.4) | async-done | bytes 524320 | tf_op jit(solution)/shard_map/all_to_all | solution.py:271
  165.8 0.7 copy.93
  166.5 1.0 reshape.79
  (51 shorter events, 0.3 us)
Async XLA Ops:
  2.7 4.4 %copy-start.22 = (s32[128]{0:T(128)S(1)}, s32[128]{0:T(128)}, u32[]{:S(2)}) copy-start(s32[128]{0:T(128)} %param.25) | copy-start | bytes 1540
  2.7 13.9 %all-to-all-start = ((bf16[4,128,4,128]{3,2,1,0:T(4,128)(2,1)}), bf16[4,128,4,128]{3,2,1,0:T(4,128)(2,1)S(1)}, u32[]{:S(2)}, u32[]{:S(2)}) async-start(bf16[4,128,4,128]{3,2,1,0:T(4,128)(2,1)} %split_columns.1), calls=%async_computation | async-start | bytes 1048576 | tf_op jit(solution)/shard_map/all_to_all | solution.py:209
  16.6 0.8 copy-start.2
  19.4 20.1 %copy-start.10 = (bf16[1,32,4096]{2,1,0:T(8,128)(2,1)S(1)}, bf16[1,32,4096]{2,1,0:T(8,128)(2,1)}, u32[]{:S(2)}) copy-start(bf16[1,32,4096]{2,1,0:T(8,128)(2,1)} %param.26) | copy-start | bytes 786436
  19.4 60.1 %all-to-all-start.1 = ((bf16[128,2,4,128]{3,2,1,0:T(4,128)(2,1)}), bf16[128,2,4,128]{3,2,1,0:T(4,128)(2,1)S(1)}, u32[]{:S(2)}, u32[]{:S(2)}) async-start(bf16[128,2,4,128]{3,2,1,0:T(4,128)(2,1)} %bitcast.69), calls=%async_computation.1 | async-start | bytes 524288 | tf_op jit(solution)/shard_map/all_to_all | solution.py:228
  38.8 0.7 copy-start.21
  40.5 8.7 %copy-start.13 = (bf16[2,128,512]{2,1,0:T(8,128)(2,1)S(1)}, bf16[2,128,512]{2,1,0:T(8,128)(2,1)}, u32[]{:S(2)}) copy-start(bf16[2,128,512]{2,1,0:T(8,128)(2,1)} %param.21) | copy-start | bytes 786436
  40.6 8.6 %copy-start.12 = (bf16[2,128,512]{2,1,0:T(8,128)(2,1)S(1)}, bf16[2,128,512]{2,1,0:T(8,128)(2,1)}, u32[]{:S(2)}) copy-start(bf16[2,128,512]{2,1,0:T(8,128)(2,1)} %param.22) | copy-start | bytes 786436
  40.6 17.2 %collective-permute-start.5 = (bf16[40,1024]{1,0:T(8,128)(2,1)S(1)}, bf16[40,1024]{1,0:T(8,128)(2,1)S(1)}, u32[]{:S(2)}, u32[]{:S(2)}) collective-permute-start(bf16[40,1024]{1,0:T(8,128)(2,1)S(1)} %bitcast.79), channel_id=1, source_target_pairs={{0,3},{1,0},{2,1},{3,2},{4,7},{5,4},{6,5},{7,6},{8,11},{9,8},{10,9... | collective-permute-start | bytes 245768 | tf_op jit(solution)/shard_map/ppermute | solution.py:177
  43.9 18.9 %collective-permute-start.4 = (bf16[40,1024]{1,0:T(8,128)(2,1)S(1)}, bf16[40,1024]{1,0:T(8,128)(2,1)S(1)}, u32[]{:S(2)}, u32[]{:S(2)}) collective-permute-start(bf16[40,1024]{1,0:T(8,128)(2,1)S(1)} %bitcast.77), channel_id=1, source_target_pairs={{0,2},{1,3},{2,0},{3,1},{4,6},{5,7},{6,4},{7,5},{8,10},{9,11},{10,... | collective-permute-start | bytes 245768 | tf_op jit(solution)/shard_map/ppermute | solution.py:177
  47.3 15.5 %collective-permute-start.3 = (bf16[40,1024]{1,0:T(8,128)(2,1)S(1)}, bf16[40,1024]{1,0:T(8,128)(2,1)S(1)}, u32[]{:S(2)}, u32[]{:S(2)}) collective-permute-start(bf16[40,1024]{1,0:T(8,128)(2,1)S(1)} %bitcast.78), channel_id=1, source_target_pairs={{0,1},{1,2},{2,3},{3,0},{4,5},{5,6},{6,7},{7,4},{8,9},{9,10},{10,1... | collective-permute-start | bytes 245768 | tf_op jit(solution)/shard_map/ppermute | solution.py:177
  49.3 15.3 %copy-start.3 = (bf16[2,2,128,512]{3,2,1,0:T(8,128)(2,1)}, bf16[2,2,128,512]{3,2,1,0:T(8,128)(2,1)S(1)}, u32[]{:S(2)}) copy-start(bf16[2,2,128,512]{3,2,1,0:T(8,128)(2,1)S(1)} %pad_maximum_fusion.own) | copy-start | bytes 1572868
  49.3 17.6 %collective-permute-start = (bf16[2,2,128,512]{3,2,1,0:T(8,128)(2,1)S(1)}, bf16[2,2,128,512]{3,2,1,0:T(8,128)(2,1)S(1)}, u32[]{:S(2)}, u32[]{:S(2)}) collective-permute-start(bf16[2,2,128,512]{3,2,1,0:T(8,128)(2,1)S(1)} %pad_maximum_fusion.own), channel_id=1, source_target_pairs={{0,1},{1,2},{2,3},{3,0},{4,5},{5,6},{6,7},{7,4},{8,9},{9,10},{10,1... | collective-permute-start | bytes 1572872 | tf_op jit(solution)/shard_map/ppermute | solution.py:177
  53.2 25.0 %collective-permute-start.1 = (bf16[2,2,128,512]{3,2,1,0:T(8,128)(2,1)S(1)}, bf16[2,2,128,512]{3,2,1,0:T(8,128)(2,1)S(1)}, u32[]{:S(2)}, u32[]{:S(2)}) collective-permute-start(bf16[2,2,128,512]{3,2,1,0:T(8,128)(2,1)S(1)} %pad_maximum_fusion.own), channel_id=1, source_target_pairs={{0,2},{1,3},{2,0},{3,1},{4,6},{5,7},{6,4},{7,5},{8,10},{9,11},{10,... | collective-permute-start | bytes 1572872 | tf_op jit(solution)/shard_map/ppermute | solution.py:177
  57.8 21.7 %collective-permute-start.2 = (bf16[2,2,128,512]{3,2,1,0:T(8,128)(2,1)S(1)}, bf16[2,2,128,512]{3,2,1,0:T(8,128)(2,1)S(1)}, u32[]{:S(2)}, u32[]{:S(2)}) collective-permute-start(bf16[2,2,128,512]{3,2,1,0:T(8,128)(2,1)S(1)} %pad_maximum_fusion.own), channel_id=1, source_target_pairs={{0,3},{1,0},{2,1},{3,2},{4,7},{5,4},{6,5},{7,6},{8,11},{9,8},{10,9... | collective-permute-start | bytes 1572872 | tf_op jit(solution)/shard_map/ppermute | solution.py:177
  61.2 0.7 copy-start.17
  62.8 0.9 copy-start.14
  62.8 1.0 copy-start.15
  62.8 1.0 copy-start.16
  66.8 13.9 %copy-start.7 = (bf16[2,2,128,512]{3,2,1,0:T(8,128)(2,1)}, bf16[2,2,128,512]{3,2,1,0:T(8,128)(2,1)S(1)}, u32[]{:S(2)}) copy-start(bf16[2,2,128,512]{3,2,1,0:T(8,128)(2,1)S(1)} %collective-permute-done.rest_0_) | copy-start | bytes 1572868
  78.2 2.6 %copy-start.8 = (bf16[2,2,128,512]{3,2,1,0:T(8,128)(2,1)}, bf16[2,2,128,512]{3,2,1,0:T(8,128)(2,1)S(1)}, u32[]{:S(2)}) copy-start(bf16[2,2,128,512]{3,2,1,0:T(8,128)(2,1)S(1)} %collective-permute-done.1.rest_1_) | copy-start | bytes 1572868
  79.6 1.2 copy-start.9
  80.8 4.7 %copy-start.18 = (f32[2,8]{1,0:T(2,128)S(1)}, f32[2,8]{1,0:T(2,128)}, u32[]{:S(2)}) copy-start(f32[2,8]{1,0:T(2,128)} %param.31) | copy-start | bytes 196
  80.8 4.7 %copy-start.19 = (f32[2,8]{1,0:T(2,128)S(1)}, f32[2,8]{1,0:T(2,128)}, u32[]{:S(2)}) copy-start(f32[2,8]{1,0:T(2,128)} %param.32) | copy-start | bytes 196
  80.8 4.7 %copy-start.20 = (f32[2,8]{1,0:T(2,128)S(1)}, f32[2,8]{1,0:T(2,128)}, u32[]{:S(2)}) copy-start(f32[2,8]{1,0:T(2,128)} %param.33) | copy-start | bytes 196
  80.8 22.0 %all-to-all-start.2 = ((bf16[4,2,512,128]{3,2,1,0:T(8,128)(2,1)}), bf16[4,2,512,128]{3,2,1,0:T(8,128)(2,1)S(1)}, u32[]{:S(2)}, u32[]{:S(2)}) async-start(bf16[4,2,512,128]{3,2,1,0:T(8,128)(2,1)} %broadcast_in_dim.5), calls=%async_computation.2 | async-start | bytes 2097152 | tf_op jit(solution)/shard_map/all_to_all | solution.py:234
  86.7 15.3 %collective-permute-start.6 = (bf16[40,1024]{1,0:T(8,128)(2,1)}, bf16[40,1024]{1,0:T(8,128)(2,1)S(1)}, u32[]{:S(2)}, u32[]{:S(2)}) collective-permute-start(bf16[40,1024]{1,0:T(8,128)(2,1)} %fusion.8), channel_id=1, source_target_pairs={{0,3},{1,0},{2,1},{3,2},{4,7},{5,4},{6,5},{7,6},{8,11},{9,8},{10,9... | collective-permute-start | bytes 245768 | tf_op jit(solution)/shard_map/ppermute | solution.py:177
  91.8 10.9 %collective-permute-start.7 = (bf16[40,1024]{1,0:T(8,128)(2,1)}, bf16[40,1024]{1,0:T(8,128)(2,1)S(1)}, u32[]{:S(2)}, u32[]{:S(2)}) collective-permute-start(bf16[40,1024]{1,0:T(8,128)(2,1)} %fusion.8), channel_id=1, source_target_pairs={{0,2},{1,3},{2,0},{3,1},{4,6},{5,7},{6,4},{7,5},{8,10},{9,11},{10,... | collective-permute-start | bytes 245768 | tf_op jit(solution)/shard_map/ppermute | solution.py:177
  94.6 31.7 %collective-permute-start.8 = (bf16[40,1024]{1,0:T(8,128)(2,1)}, bf16[40,1024]{1,0:T(8,128)(2,1)S(1)}, u32[]{:S(2)}, u32[]{:S(2)}) collective-permute-start(bf16[40,1024]{1,0:T(8,128)(2,1)} %fusion.8), channel_id=1, source_target_pairs={{0,1},{1,2},{2,3},{3,0},{4,5},{5,6},{6,7},{7,4},{8,9},{9,10},{10,1... | collective-permute-start | bytes 245768 | tf_op jit(solution)/shard_map/ppermute | solution.py:177
  102.8 1.0 copy-start
  110.2 38.6 %all-to-all-start.3 = ((bf16[128,2,4,128]{3,2,1,0:T(4,128)(2,1)}), bf16[128,2,4,128]{3,2,1,0:T(4,128)(2,1)S(1)}, u32[]{:S(2)}, u32[]{:S(2)}) async-start(bf16[128,2,4,128]{3,2,1,0:T(4,128)(2,1)} %bitcast.55), calls=%async_computation.3 | async-start | bytes 524288 | tf_op jit(solution)/shard_map/all_to_all | solution.py:242
  126.3 1.5 copy-start.1
  148.8 0.7 copy-start.4
  151.8 4.2 %copy-start.5 = (f32[2,128,512]{2,1,0:T(8,128)S(1)}, f32[2,128,512]{2,1,0:T(8,128)}, u32[]{:S(2)}) copy-start(f32[2,128,512]{2,1,0:T(8,128)} %param.19) | copy-start | bytes 1572868
  151.8 14.0 %all-to-all-start.4 = ((bf16[4,128,4,128]{3,2,1,0:T(4,128)(2,1)}), bf16[4,128,4,128]{3,2,1,0:T(4,128)(2,1)S(1)}, u32[]{:S(2)}, u32[]{:S(2)}) async-start(bf16[4,128,4,128]{3,2,1,0:T(4,128)(2,1)} %get-tuple-element.31), calls=%async_computation.4 | async-start | bytes 1048576 | tf_op jit(solution)/shard_map/all_to_all | solution.py:271
  156.0 1.2 copy-start.11
  156.0 1.9 %copy-start.6 = (f32[2,128,512]{2,1,0:T(8,128)S(1)}, f32[2,128,512]{2,1,0:T(8,128)}, u32[]{:S(2)}) copy-start(f32[2,128,512]{2,1,0:T(8,128)} %param.20) | copy-start | bytes 1572868

commit v2 on v1

--- a/solution.py
+++ b/solution.py
@@ -106,18 +106,20 @@
         ratio = jnp.sqrt(adam_total) / (jnp.sqrt(shampoo_total) + graft_eps)
         for k in range(ways):
             member = lax.rem(here[0] - k + ways, ways)
-            update[slot, pl.ds(member * quarter, quarter), :] = (
-                shampoo[k * quarter : (k + 1) * quarter, :quarter] * ratio
+            part = shampoo[k * quarter : (k + 1) * quarter, :quarter] * ratio
+            owners_here = quarter // update.shape[2]
+            update[pl.ds(member * owners_here, owners_here), slot] = part.reshape(
+                owners_here, update.shape[2], quarter
             ).astype(low)
 
 
-def precondition(here, columns, factors, row_old, col_old):
+def precondition(here, columns, factors, row_old, col_old, rows_dev):
     _, slot_count, side, quarter = columns.shape
     vmem = pl.BlockSpec(memory_space=pltpu.VMEM)
     return pl.pallas_call(
         functools.partial(core_kernel, slot_count=slot_count),
         out_shape=(
-            jax.ShapeDtypeStruct((slot_count, side, quarter), low),
+            jax.ShapeDtypeStruct((side // rows_dev, slot_count, rows_dev, quarter), low),
             jax.ShapeDtypeStruct((side, slot_count), full),
             jax.ShapeDtypeStruct((slot_count, side), full),
         ),
@@ -208,6 +210,9 @@
     wo_parts = split_columns(wo_grads.reshape(block_count, rows_dev, side), ways)
     wo_terms = lax.all_to_all(wo_parts, "tensor", 0, 0, tiled=True)
 
+    roots = jnp.stack([left_roots, right_roots])
+    factors = from_peers(lambda k: roots, "tensor")
+
     emb_rows, emb_cols = emb_master.shape
     gain_rows, gain_cols = gain_master.shape
     pad_rows = 8
@@ -226,19 +231,15 @@
     outgoing = place_blocks(slot_of, wo_terms, owner_count * slot_count)
     outgoing = outgoing.reshape(owner_count, slot_count, rows_dev, quarter)
     own_cols = lax.all_to_all(outgoing, "shard", 0, 0, tiled=True)
-    roots = jnp.stack([left_roots, right_roots])
-    factors = from_peers(lambda k: roots, "tensor")
-
-    own_cols, factors = lax.optimization_barrier((own_cols, factors))
+    own_cols, factors, small_sum = lax.optimization_barrier((own_cols, factors, small_sum))
     own_cols = own_cols.transpose(1, 0, 2, 3).reshape(slot_count, side, quarter)
     gathered = lax.all_to_all(
         jnp.broadcast_to(own_cols[None], (ways,) + own_cols.shape), "tensor", 0, 0, tiled=True
     )
     update, row_new, col_new = precondition(
-        here.reshape(1).astype(jnp.int32), gathered, factors, row_moments.T, col_moments
+        here.reshape(1).astype(jnp.int32), gathered, factors, row_moments.T, col_moments, rows_dev
     )
     row_new = row_new.T
-    update = update.reshape(slot_count, owner_count, rows_dev, quarter).transpose(1, 0, 2, 3)
     returned = lax.all_to_all(update, "shard", 0, 0, tiled=True)
 
     block = gathered.transpose(1, 2, 0, 3).reshape(slot_count, side, side)
@@ -269,7 +270,8 @@
         ways,
     )
     wo_low = lax.all_to_all(wo_low, "tensor", 0, 0, tiled=True)
-    wo_weights = wo_low.transpose(1, 2, 0, 3).reshape(wo_master.shape[:3] + (rows_dev, side))
+    wo_weights = jnp.concatenate([wo_low[member] for member in range(ways)], axis=-1)
+    wo_weights = wo_weights.reshape(wo_master.shape[:3] + (rows_dev, side))
     return (
         wo_new.reshape(wo_master.shape),
         wo_weights,

time: 168 us -> 165 us (0.982)
  starting transfers between devices: 79.7 us -> 76.1 us
  waiting for transfers between devices: 56.3 us -> 54.3 us
    all_to_all x1, waiting for transfers between devices: 20.5 us -> 15.8 us  [per_device(): returned = lax.all_to_all(update, 'shard', 0, 0, tiled=True)]
    ppermute x9, waiting for transfers between devices: 20.3 us -> 22.9 us  [from_peers(): lax.ppermute(value, axis, [(i, (i + k) % count) for i in range(count)])]
    ppermute x9, starting transfers between devices: 31 us -> 29 us  [from_peers(): lax.ppermute(value, axis, [(i, (i + k) % count) for i in range(count)])]
    reshape x1 -> x0, local copies, waits for them, and re-layouts: 1.74 us -> none  [per_device(): update.reshape(slot_count, owner_count, rows_dev, quarter)]
  transfers between devices with their start and end apart: 14 -> 14, of which waited for: 8 -> 7; matrix products, arithmetic and copies ran while one was open for 7% -> 9% of each run, Pallas kernels for 3% -> 3%
where the time goes in v2:
time: 165 us; the launch traced here: 164 us
  starting transfers between devices  76.1 us (46%)
  waiting for transfers between devices  54.3 us (33%)
  local copies, waits for them, and re-layouts  14.5 us (9%)
  Pallas kernels  11.1 us (7%)
  other arithmetic  4.78 us (3%)
  matrix products  2.43 us (1%)
    ppermute x9, starting transfers between devices, from_peers(): lax.ppermute(value, axis, [(i, (i + k) % count) for i in range(count)])  29 us
    ppermute x9, waiting for transfers between devices, from_peers(): lax.ppermute(value, axis, [(i, (i + k) % count) for i in range(count)])  22.9 us
    all_to_all x1, starting transfers between devices, per_device(): own_cols = lax.all_to_all(outgoing, 'shard', 0, 0, tiled=True)  19.3 us
    all_to_all x1, starting transfers between devices, per_device(): returned = lax.all_to_all(update, 'shard', 0, 0, tiled=True)  16.1 us
    all_to_all x1, waiting for transfers between devices, per_device(): returned = lax.all_to_all(update, 'shard', 0, 0, tiled=True)  15.8 us
    unnamed x59, local copies, waits for them, and re-layouts  9.4 us
    all_to_all x1, waiting for transfers between devices, per_device(): wo_terms = lax.all_to_all(wo_parts, 'tensor', 0, 0, tiled=True)  8.77 us
    all_to_all x1, waiting for transfers between devices, per_device(): wo_low = lax.all_to_all(wo_low, 'tensor', 0, 0, tiled=True)  6.91 us
  transfers between devices with their start and end apart: 14, of which 7 were waited for; matrix products, arithmetic and copies ran while one was open for 9% of the time, Pallas kernels for 3%

profile of v2, /device:TPU:32, one launch (start us, length us, event | category | flops | bytes accessed | tf_op | source)
XLA Modules:
  0.0 164.3 jit_solution(14077995291200683471)
XLA Ops:
  0.6 2.0 %split_columns.1 = bf16[4,128,4,128]{3,2,1,0:T(4,128)(2,1)} custom-call(bf16[128,4,512]{2,1,0:T(4,128)(2,1)} %bitcast.66), custom_call_target="tpu_custom_call" | custom-call | tf_op jit(solution)/shard_map/split_columns/pallas_call | solution.py:41
  2.7 4.4 %all-to-all-start = ((bf16[4,128,4,128]{3,2,1,0:T(4,128)(2,1)}), bf16[4,128,4,128]{3,2,1,0:T(4,128)(2,1)S(1)}, u32[]{:S(2)}, u32[]{:S(2)}) async-start(bf16[4,128,4,128]{3,2,1,0:T(4,128)(2,1)} %split_columns.1), calls=%async_computation | async-start | bytes 1048576 | tf_op jit(solution)/shard_map/all_to_all | solution.py:211
  7.1 0.2 convert_reduce_fusion
  7.3 0.5 multiply_add_fusion.2.slot_of
  7.8 8.8 %all-to-all-done.terms = bf16[4,128,4,128]{3,2,1,0:T(4,128)(2,1)S(1)} async-done(((bf16[4,128,4,128]{3,2,1,0:T(4,128)(2,1)}), bf16[4,128,4,128]{3,2,1,0:T(4,128)(2,1)S(1)}, u32[]{:S(2)}, u32[]{:S(2)}) %all-to-all-start) | async-done | bytes 524320 | tf_op jit(solution)/shard_map/all_to_all | solution.py:211
  16.6 0.8 copy-done.2
  17.4 2.1 %place_blocks.1 = bf16[256,4,128]{2,1,0:T(4,128)(2,1)} custom-call(s32[128]{0:T(128)} %multiply_add_fusion.2.slot_of, bf16[4,128,4,128]{3,2,1,0:T(4,128)(2,1)} %copy-done.2), custom_call_target="tpu_custom_call" | custom-call | tf_op jit(solution)/shard_map/place_blocks/pallas_call | solution.py:66
  19.4 19.3 %all-to-all-start.1 = ((bf16[128,2,4,128]{3,2,1,0:T(4,128)(2,1)}), bf16[128,2,4,128]{3,2,1,0:T(4,128)(2,1)S(1)}, u32[]{:S(2)}, u32[]{:S(2)}) async-start(bf16[128,2,4,128]{3,2,1,0:T(4,128)(2,1)} %bitcast.65), calls=%async_computation.1 | async-start | bytes 524288 | tf_op jit(solution)/shard_map/all_to_all | solution.py:233
  38.8 0.0 copy-start.10
  38.8 0.1 pad_maximum_fusion.own
  38.9 2.5 %collective-permute-start = (bf16[2,2,128,512]{3,2,1,0:T(8,128)(2,1)S(1)}, bf16[2,2,128,512]{3,2,1,0:T(8,128)(2,1)S(1)}, u32[]{:S(2)}, u32[]{:S(2)}) collective-permute-start(bf16[2,2,128,512]{3,2,1,0:T(8,128)(2,1)S(1)} %pad_maximum_fusion.own), channel_id=1, source_target_pairs={{0,1},{1,2},{2,3},{3,0},{4,5},{5,6},{6,7},{7,4},{8,9},{9,10},{10,1... | collective-permute-start | bytes 1572872 | tf_op jit(solution)/shard_map/ppermute | solution.py:179
  41.3 4.0 %collective-permute-start.1 = (bf16[2,2,128,512]{3,2,1,0:T(8,128)(2,1)S(1)}, bf16[2,2,128,512]{3,2,1,0:T(8,128)(2,1)S(1)}, u32[]{:S(2)}, u32[]{:S(2)}) collective-permute-start(bf16[2,2,128,512]{3,2,1,0:T(8,128)(2,1)S(1)} %pad_maximum_fusion.own), channel_id=1, source_target_pairs={{0,2},{1,3},{2,0},{3,1},{4,6},{5,7},{6,4},{7,5},{8,10},{9,11},{10,... | collective-permute-start | bytes 1572872 | tf_op jit(solution)/shard_map/ppermute | solution.py:179
  45.3 2.5 %collective-permute-start.2 = (bf16[2,2,128,512]{3,2,1,0:T(8,128)(2,1)S(1)}, bf16[2,2,128,512]{3,2,1,0:T(8,128)(2,1)S(1)}, u32[]{:S(2)}, u32[]{:S(2)}) collective-permute-start(bf16[2,2,128,512]{3,2,1,0:T(8,128)(2,1)S(1)} %pad_maximum_fusion.own), channel_id=1, source_target_pairs={{0,3},{1,0},{2,1},{3,2},{4,7},{5,4},{6,5},{7,6},{8,11},{9,8},{10,9... | collective-permute-start | bytes 1572872 | tf_op jit(solution)/shard_map/ppermute | solution.py:179
  47.9 0.0 copy-start.22
  47.9 0.6 copy-done.22
  48.6 0.1 reshape_squeeze.7
  48.6 0.2 reshape_squeeze.6
  48.9 0.1 fusion.1
  49.0 0.6 constant_dynamic-slice_fusion.2
  49.7 3.3 %collective-permute-start.5 = (bf16[40,1024]{1,0:T(8,128)(2,1)S(1)}, bf16[40,1024]{1,0:T(8,128)(2,1)S(1)}, u32[]{:S(2)}, u32[]{:S(2)}) collective-permute-start(bf16[40,1024]{1,0:T(8,128)(2,1)S(1)} %bitcast.78), channel_id=1, source_target_pairs={{0,3},{1,0},{2,1},{3,2},{4,7},{5,4},{6,5},{7,6},{8,11},{9,8},{10,9... | collective-permute-start | bytes 245768 | tf_op jit(solution)/shard_map/ppermute | solution.py:179
  53.1 4.0 %collective-permute-start.4 = (bf16[40,1024]{1,0:T(8,128)(2,1)S(1)}, bf16[40,1024]{1,0:T(8,128)(2,1)S(1)}, u32[]{:S(2)}, u32[]{:S(2)}) collective-permute-start(bf16[40,1024]{1,0:T(8,128)(2,1)S(1)} %bitcast.76), channel_id=1, source_target_pairs={{0,2},{1,3},{2,0},{3,1},{4,6},{5,7},{6,4},{7,5},{8,10},{9,11},{10,... | collective-permute-start | bytes 245768 | tf_op jit(solution)/shard_map/ppermute | solution.py:179
  57.1 15.2 %collective-permute-done.5 = bf16[40,1024]{1,0:T(8,128)(2,1)S(1)} collective-permute-done((bf16[40,1024]{1,0:T(8,128)(2,1)S(1)}, bf16[40,1024]{1,0:T(8,128)(2,1)S(1)}, u32[]{:S(2)}, u32[]{:S(2)}) %collective-permute-start.5) | collective-permute-done | bytes 81952 | tf_op jit(solution)/shard_map/ppermute | solution.py:179
  72.3 2.1 %collective-permute-start.3 = (bf16[40,1024]{1,0:T(8,128)(2,1)S(1)}, bf16[40,1024]{1,0:T(8,128)(2,1)S(1)}, u32[]{:S(2)}, u32[]{:S(2)}) collective-permute-start(bf16[40,1024]{1,0:T(8,128)(2,1)S(1)} %bitcast.77), channel_id=1, source_target_pairs={{0,1},{1,2},{2,3},{3,0},{4,5},{5,6},{6,7},{7,4},{8,9},{9,10},{10,1... | collective-permute-start | bytes 245768 | tf_op jit(solution)/shard_map/ppermute | solution.py:179
  74.4 0.0 copy-start.18
  74.4 0.7 copy-done.18
  75.1 0.9 copy.68
  76.0 3.9 %collective-permute-done.3 = bf16[40,1024]{1,0:T(8,128)(2,1)S(1)} collective-permute-done((bf16[40,1024]{1,0:T(8,128)(2,1)S(1)}, bf16[40,1024]{1,0:T(8,128)(2,1)S(1)}, u32[]{:S(2)}, u32[]{:S(2)}) %collective-permute-start.3) | collective-permute-done | bytes 81952 | tf_op jit(solution)/shard_map/ppermute | solution.py:179
  79.8 0.1 fusion.4
  79.9 0.0 copy-start.8
  80.0 0.1 copy.67
  80.1 1.4 broadcast_in_dim.5
  81.5 3.7 %all-to-all-start.2 = ((bf16[4,2,512,128]{3,2,1,0:T(8,128)(2,1)}), bf16[4,2,512,128]{3,2,1,0:T(8,128)(2,1)S(1)}, u32[]{:S(2)}, u32[]{:S(2)}) async-start(bf16[4,2,512,128]{3,2,1,0:T(8,128)(2,1)} %broadcast_in_dim.5), calls=%async_computation.2 | async-start | bytes 2097152 | tf_op jit(solution)/shard_map/all_to_all | solution.py:236
  85.2 0.9 copy-done.15
  86.0 0.1 copy-done.16
  86.1 0.8 fusion.11
  86.9 0.6 fusion.13
  87.5 5.1 %collective-permute-start.6 = (bf16[40,1024]{1,0:T(8,128)(2,1)S(1)}, bf16[40,1024]{1,0:T(8,128)(2,1)S(1)}, u32[]{:S(2)}, u32[]{:S(2)}) collective-permute-start(bf16[40,1024]{1,0:T(8,128)(2,1)S(1)} %fusion.7), channel_id=1, source_target_pairs={{0,3},{1,0},{2,1},{3,2},{4,7},{5,4},{6,5},{7,6},{8,11},{9,8},{10,9... | collective-permute-start | bytes 245768 | tf_op jit(solution)/shard_map/ppermute | solution.py:179
  92.6 2.8 %collective-permute-start.7 = (bf16[40,1024]{1,0:T(8,128)(2,1)S(1)}, bf16[40,1024]{1,0:T(8,128)(2,1)S(1)}, u32[]{:S(2)}, u32[]{:S(2)}) collective-permute-start(bf16[40,1024]{1,0:T(8,128)(2,1)S(1)} %fusion.7), channel_id=1, source_target_pairs={{0,2},{1,3},{2,0},{3,1},{4,6},{5,7},{6,4},{7,5},{8,10},{9,11},{10,... | collective-permute-start | bytes 245768 | tf_op jit(solution)/shard_map/ppermute | solution.py:179
  95.4 2.8 %collective-permute-start.8 = (bf16[40,1024]{1,0:T(8,128)(2,1)S(1)}, bf16[40,1024]{1,0:T(8,128)(2,1)S(1)}, u32[]{:S(2)}, u32[]{:S(2)}) collective-permute-start(bf16[40,1024]{1,0:T(8,128)(2,1)S(1)} %fusion.7), channel_id=1, source_target_pairs={{0,1},{1,2},{2,3},{3,0},{4,5},{5,6},{6,7},{7,4},{8,9},{9,10},{10,1... | collective-permute-start | bytes 245768 | tf_op jit(solution)/shard_map/ppermute | solution.py:179
  98.2 2.1 %collective-permute-done.6 = bf16[40,1024]{1,0:T(8,128)(2,1)S(1)} collective-permute-done((bf16[40,1024]{1,0:T(8,128)(2,1)S(1)}, bf16[40,1024]{1,0:T(8,128)(2,1)S(1)}, u32[]{:S(2)}, u32[]{:S(2)}) %collective-permute-start.6) | collective-permute-done | bytes 81952 | tf_op jit(solution)/shard_map/ppermute | solution.py:179
  100.3 1.6 collective-permute-done.7
  101.9 1.0 copy-done
  103.0 4.8 %precondition.1 = (bf16[128,2,4,128]{3,2,1,0:T(4,128)(2,1)}, f32[512,2]{1,0:T(8,128)}, f32[2,512]{1,0:T(2,128)}) custom-call(s32[1]{0:T(128)} %bitcast.here, bf16[4,2,512,128]{3,2,1,0:T(8,128)(2,1)} %copy-done, bf16[2,2,128,512]{3,2,1,0:T(8,128)(2,1)} %copy-done.3, bf16[2,2,128,512]{3,2,1,0:T(8,128)(2,1)} %copy-done.7, bf16[2,2,128,512]{3,2,1,0:T(8,128)(2,1)} %copy-done.8, ...), custom_call_target="tpu_custom_call" | custom-call | tf_op jit(solution)/shard_map/precondition/pallas_call | solution.py:119
  107.7 16.1 %all-to-all-start.3 = ((bf16[128,2,4,128]{3,2,1,0:T(4,128)(2,1)}), bf16[128,2,4,128]{3,2,1,0:T(4,128)(2,1)S(1)}, u32[]{:S(2)}, u32[]{:S(2)}) async-start(bf16[128,2,4,128]{3,2,1,0:T(4,128)(2,1)} %get-tuple-element.30), calls=%async_computation.3 | async-start | bytes 524288 | tf_op jit(solution)/shard_map/all_to_all | solution.py:243
  123.9 0.6 bitcast_dynamic-update-slice_fusion
  124.5 0.6 bitcast_dynamic-update-slice_fusion.7
  125.1 0.6 bitcast_dynamic-update-slice_fusion.5
  125.8 0.6 bitcast_dynamic-update-slice_fusion.3
  126.4 0.6 bitcast_dynamic-update-slice_fusion.1
  127.0 1.0 dynamic-slice_bitcast_fusion
  128.0 0.7 copy.85
  128.7 0.7 dynamic-slice_bitcast_fusion.1
  129.4 0.6 reshape.78
  130.0 0.5 copy.69
  130.6 15.8 %all-to-all-done.3 = bf16[128,2,4,128]{3,2,1,0:T(4,128)(2,1)S(1)} async-done(((bf16[128,2,4,128]{3,2,1,0:T(4,128)(2,1)}), bf16[128,2,4,128]{3,2,1,0:T(4,128)(2,1)S(1)}, u32[]{:S(2)}, u32[]{:S(2)}) %all-to-all-start.3) | async-done | bytes 262176 | tf_op jit(solution)/shard_map/all_to_all | solution.py:243
  146.3 0.7 copy-done.4
  147.0 2.3 %apply_updates.1 = (f32[128,4,128]{2,1,0:T(4,128)}, bf16[4,128,4,128]{3,2,1,0:T(4,128)(2,1)}) custom-call(s32[128]{0:T(128)} %multiply_add_fusion.2.slot_of, bf16[256,4,128]{2,1,0:T(4,128)(2,1)} %bitcast.62, f32[128,4,128]{2,1,0:T(4,128)} %bitcast.71), custom_call_target="tpu_custom_call" | custom-call | tf_op jit(solution)/shard_map/apply_updates/pallas_call | solution.py:148
  149.3 3.6 %all-to-all-start.4 = ((bf16[4,128,4,128]{3,2,1,0:T(4,128)(2,1)}), bf16[4,128,4,128]{3,2,1,0:T(4,128)(2,1)S(1)}, u32[]{:S(2)}, u32[]{:S(2)}) async-start(bf16[4,128,4,128]{3,2,1,0:T(4,128)(2,1)} %get-tuple-element.32), calls=%async_computation.4 | async-start | bytes 1048576 | tf_op jit(solution)/shard_map/all_to_all | solution.py:272
  152.9 1.1 convolution_add_fusion.1
  154.1 0.7 copy.76
  154.8 1.3 convolution_add_fusion
  156.1 6.9 %all-to-all-done.4 = bf16[4,128,4,128]{3,2,1,0:T(4,128)(2,1)S(1)} async-done(((bf16[4,128,4,128]{3,2,1,0:T(4,128)(2,1)}), bf16[4,128,4,128]{3,2,1,0:T(4,128)(2,1)S(1)}, u32[]{:S(2)}, u32[]{:S(2)}) %all-to-all-start.4) | async-done | bytes 524320 | tf_op jit(solution)/shard_map/all_to_all | solution.py:272
  163.0 0.2 fusion.15
  163.2 1.2 pad_maximum_fusion.1
  (53 shorter events, 0.2 us)
Async XLA Ops:
  2.7 4.4 %copy-start.23 = (s32[128]{0:T(128)S(1)}, s32[128]{0:T(128)}, u32[]{:S(2)}) copy-start(s32[128]{0:T(128)} %param.25) | copy-start | bytes 1540
  2.7 13.9 %all-to-all-start = ((bf16[4,128,4,128]{3,2,1,0:T(4,128)(2,1)}), bf16[4,128,4,128]{3,2,1,0:T(4,128)(2,1)S(1)}, u32[]{:S(2)}, u32[]{:S(2)}) async-start(bf16[4,128,4,128]{3,2,1,0:T(4,128)(2,1)} %split_columns.1), calls=%async_computation | async-start | bytes 1048576 | tf_op jit(solution)/shard_map/all_to_all | solution.py:211
  16.6 0.8 copy-start.2
  19.4 19.3 %copy-start.12 = (bf16[2,128,512]{2,1,0:T(8,128)(2,1)S(1)}, bf16[2,128,512]{2,1,0:T(8,128)(2,1)}, u32[]{:S(2)}) copy-start(bf16[2,128,512]{2,1,0:T(8,128)(2,1)} %param.22) | copy-start | bytes 786436
  19.4 19.3 %copy-start.13 = (bf16[2,128,512]{2,1,0:T(8,128)(2,1)S(1)}, bf16[2,128,512]{2,1,0:T(8,128)(2,1)}, u32[]{:S(2)}) copy-start(bf16[2,128,512]{2,1,0:T(8,128)(2,1)} %param.21) | copy-start | bytes 786436
  19.4 60.5 %all-to-all-start.1 = ((bf16[128,2,4,128]{3,2,1,0:T(4,128)(2,1)}), bf16[128,2,4,128]{3,2,1,0:T(4,128)(2,1)S(1)}, u32[]{:S(2)}, u32[]{:S(2)}) async-start(bf16[128,2,4,128]{3,2,1,0:T(4,128)(2,1)} %bitcast.65), calls=%async_computation.1 | async-start | bytes 524288 | tf_op jit(solution)/shard_map/all_to_all | solution.py:233
  38.8 9.9 %copy-start.10 = (bf16[1,32,4096]{2,1,0:T(8,128)(2,1)S(1)}, bf16[1,32,4096]{2,1,0:T(8,128)(2,1)}, u32[]{:S(2)}) copy-start(bf16[1,32,4096]{2,1,0:T(8,128)(2,1)} %param.26) | copy-start | bytes 786436
  38.8 10.2 %copy-start.3 = (bf16[2,2,128,512]{3,2,1,0:T(8,128)(2,1)}, bf16[2,2,128,512]{3,2,1,0:T(8,128)(2,1)S(1)}, u32[]{:S(2)}) copy-start(bf16[2,2,128,512]{3,2,1,0:T(8,128)(2,1)S(1)} %pad_maximum_fusion.own) | copy-start | bytes 1572868
  38.9 41.0 %collective-permute-start = (bf16[2,2,128,512]{3,2,1,0:T(8,128)(2,1)S(1)}, bf16[2,2,128,512]{3,2,1,0:T(8,128)(2,1)S(1)}, u32[]{:S(2)}, u32[]{:S(2)}) collective-permute-start(bf16[2,2,128,512]{3,2,1,0:T(8,128)(2,1)S(1)} %pad_maximum_fusion.own), channel_id=1, source_target_pairs={{0,1},{1,2},{2,3},{3,0},{4,5},{5,6},{6,7},{7,4},{8,9},{9,10},{10,1... | collective-permute-start | bytes 1572872 | tf_op jit(solution)/shard_map/ppermute | solution.py:179
  41.3 38.6 %collective-permute-start.1 = (bf16[2,2,128,512]{3,2,1,0:T(8,128)(2,1)S(1)}, bf16[2,2,128,512]{3,2,1,0:T(8,128)(2,1)S(1)}, u32[]{:S(2)}, u32[]{:S(2)}) collective-permute-start(bf16[2,2,128,512]{3,2,1,0:T(8,128)(2,1)S(1)} %pad_maximum_fusion.own), channel_id=1, source_target_pairs={{0,2},{1,3},{2,0},{3,1},{4,6},{5,7},{6,4},{7,5},{8,10},{9,11},{10,... | collective-permute-start | bytes 1572872 | tf_op jit(solution)/shard_map/ppermute | solution.py:179
  45.3 34.6 %collective-permute-start.2 = (bf16[2,2,128,512]{3,2,1,0:T(8,128)(2,1)S(1)}, bf16[2,2,128,512]{3,2,1,0:T(8,128)(2,1)S(1)}, u32[]{:S(2)}, u32[]{:S(2)}) collective-permute-start(bf16[2,2,128,512]{3,2,1,0:T(8,128)(2,1)S(1)} %pad_maximum_fusion.own), channel_id=1, source_target_pairs={{0,3},{1,0},{2,1},{3,2},{4,7},{5,4},{6,5},{7,6},{8,11},{9,8},{10,9... | collective-permute-start | bytes 1572872 | tf_op jit(solution)/shard_map/ppermute | solution.py:179
  47.9 0.7 copy-start.22
  49.7 22.6 %collective-permute-start.5 = (bf16[40,1024]{1,0:T(8,128)(2,1)S(1)}, bf16[40,1024]{1,0:T(8,128)(2,1)S(1)}, u32[]{:S(2)}, u32[]{:S(2)}) collective-permute-start(bf16[40,1024]{1,0:T(8,128)(2,1)S(1)} %bitcast.78), channel_id=1, source_target_pairs={{0,3},{1,0},{2,1},{3,2},{4,7},{5,4},{6,5},{7,6},{8,11},{9,8},{10,9... | collective-permute-start | bytes 245768 | tf_op jit(solution)/shard_map/ppermute | solution.py:179
  53.1 22.9 %collective-permute-start.4 = (bf16[40,1024]{1,0:T(8,128)(2,1)S(1)}, bf16[40,1024]{1,0:T(8,128)(2,1)S(1)}, u32[]{:S(2)}, u32[]{:S(2)}) collective-permute-start(bf16[40,1024]{1,0:T(8,128)(2,1)S(1)} %bitcast.76), channel_id=1, source_target_pairs={{0,2},{1,3},{2,0},{3,1},{4,6},{5,7},{6,4},{7,5},{8,10},{9,11},{10,... | collective-permute-start | bytes 245768 | tf_op jit(solution)/shard_map/ppermute | solution.py:179
  72.3 7.5 %collective-permute-start.3 = (bf16[40,1024]{1,0:T(8,128)(2,1)S(1)}, bf16[40,1024]{1,0:T(8,128)(2,1)S(1)}, u32[]{:S(2)}, u32[]{:S(2)}) collective-permute-start(bf16[40,1024]{1,0:T(8,128)(2,1)S(1)} %bitcast.77), channel_id=1, source_target_pairs={{0,1},{1,2},{2,3},{3,0},{4,5},{5,6},{6,7},{7,4},{8,9},{9,10},{10,1... | collective-permute-start | bytes 245768 | tf_op jit(solution)/shard_map/ppermute | solution.py:179
  74.4 0.7 copy-start.18
  79.9 1.5 copy-start.7
  79.9 1.5 copy-start.8
  80.0 1.5 copy-start.9
  81.4 3.7 %copy-start.17 = (f32[32,1024]{1,0:T(8,128)S(1)}, f32[32,1024]{1,0:T(8,128)}, u32[]{:S(2)}) copy-start(f32[32,1024]{1,0:T(8,128)} %param.29) | copy-start | bytes 393220
  81.5 20.5 %all-to-all-start.2 = ((bf16[4,2,512,128]{3,2,1,0:T(8,128)(2,1)}), bf16[4,2,512,128]{3,2,1,0:T(8,128)(2,1)S(1)}, u32[]{:S(2)}, u32[]{:S(2)}) async-start(bf16[4,2,512,128]{3,2,1,0:T(8,128)(2,1)} %broadcast_in_dim.5), calls=%async_computation.2 | async-start | bytes 2097152 | tf_op jit(solution)/shard_map/all_to_all | solution.py:236
  85.1 0.9 copy-start.15
  85.1 1.0 copy-start.16
  86.1 0.8 copy-start.19
  86.1 0.8 copy-start.20
  86.1 0.8 copy-start.21
  87.5 12.8 %collective-permute-start.6 = (bf16[40,1024]{1,0:T(8,128)(2,1)S(1)}, bf16[40,1024]{1,0:T(8,128)(2,1)S(1)}, u32[]{:S(2)}, u32[]{:S(2)}) collective-permute-start(bf16[40,1024]{1,0:T(8,128)(2,1)S(1)} %fusion.7), channel_id=1, source_target_pairs={{0,3},{1,0},{2,1},{3,2},{4,7},{5,4},{6,5},{7,6},{8,11},{9,8},{10,9... | collective-permute-start | bytes 245768 | tf_op jit(solution)/shard_map/ppermute | solution.py:179
  92.6 9.3 %collective-permute-start.7 = (bf16[40,1024]{1,0:T(8,128)(2,1)S(1)}, bf16[40,1024]{1,0:T(8,128)(2,1)S(1)}, u32[]{:S(2)}, u32[]{:S(2)}) collective-permute-start(bf16[40,1024]{1,0:T(8,128)(2,1)S(1)} %fusion.7), channel_id=1, source_target_pairs={{0,2},{1,3},{2,0},{3,1},{4,6},{5,7},{6,4},{7,5},{8,10},{9,11},{10,... | collective-permute-start | bytes 245768 | tf_op jit(solution)/shard_map/ppermute | solution.py:179
  95.4 28.5 %collective-permute-start.8 = (bf16[40,1024]{1,0:T(8,128)(2,1)S(1)}, bf16[40,1024]{1,0:T(8,128)(2,1)S(1)}, u32[]{:S(2)}, u32[]{:S(2)}) collective-permute-start(bf16[40,1024]{1,0:T(8,128)(2,1)S(1)} %fusion.7), channel_id=1, source_target_pairs={{0,1},{1,2},{2,3},{3,0},{4,5},{5,6},{6,7},{7,4},{8,9},{9,10},{10,1... | collective-permute-start | bytes 245768 | tf_op jit(solution)/shard_map/ppermute | solution.py:179
  101.9 5.8 %copy-start.14 = (bf16[8,40,1024]{2,1,0:T(8,128)(2,1)}, bf16[8,40,1024]{2,1,0:T(8,128)(2,1)S(1)}, u32[]{:S(2)}) copy-start(bf16[8,40,1024]{2,1,0:T(8,128)(2,1)S(1)} %bitcast_dynamic-update-slice_fusion.2) | copy-start | bytes 1966084
  101.9 1.0 copy-start
  107.7 38.6 %all-to-all-start.3 = ((bf16[128,2,4,128]{3,2,1,0:T(4,128)(2,1)}), bf16[128,2,4,128]{3,2,1,0:T(4,128)(2,1)S(1)}, u32[]{:S(2)}, u32[]{:S(2)}) async-start(bf16[128,2,4,128]{3,2,1,0:T(4,128)(2,1)} %get-tuple-element.30), calls=%async_computation.3 | async-start | bytes 524288 | tf_op jit(solution)/shard_map/all_to_all | solution.py:243
  123.8 6.2 %copy-start.1 = (bf16[4,2,512,128]{3,2,1,0:T(8,128)(2,1)S(1)}, bf16[4,2,512,128]{3,2,1,0:T(8,128)(2,1)}, u32[]{:S(2)}) copy-start(bf16[4,2,512,128]{3,2,1,0:T(8,128)(2,1)} %copy-done) | copy-start | bytes 3145732
  146.3 0.7 copy-start.4
  149.3 3.6 %copy-start.5 = (f32[2,128,512]{2,1,0:T(8,128)S(1)}, f32[2,128,512]{2,1,0:T(8,128)}, u32[]{:S(2)}) copy-start(f32[2,128,512]{2,1,0:T(8,128)} %param.19) | copy-start | bytes 1572868
  149.3 13.7 %all-to-all-start.4 = ((bf16[4,128,4,128]{3,2,1,0:T(4,128)(2,1)}), bf16[4,128,4,128]{3,2,1,0:T(4,128)(2,1)S(1)}, u32[]{:S(2)}, u32[]{:S(2)}) async-start(bf16[4,128,4,128]{3,2,1,0:T(4,128)(2,1)} %get-tuple-element.32), calls=%async_computation.4 | async-start | bytes 1048576 | tf_op jit(solution)/shard_map/all_to_all | solution.py:272
  152.9 1.2 copy-start.11
  152.9 1.9 %copy-start.6 = (f32[2,128,512]{2,1,0:T(8,128)S(1)}, f32[2,128,512]{2,1,0:T(8,128)}, u32[]{:S(2)}) copy-start(f32[2,128,512]{2,1,0:T(8,128)} %param.20) | copy-start | bytes 1572868

commit v3 on v2

--- a/solution.py
+++ b/solution.py
@@ -157,6 +157,10 @@
     )(slot_of, updates, master)
 
 
+def in_vmem(value):
+    return pltpu.with_memory_space_constraint(value, pltpu.VMEM)
+
+
 def slots_of(owners, slot_count):
     ids = jnp.arange(owners.shape[0], dtype=jnp.int32)
     earlier = (owners[:, None] == owners[None, :]) & (ids[None, :] < ids[:, None])
@@ -228,16 +232,16 @@
     )
     small_sum = sum(piece.astype(full) for piece in small_pieces)
 
-    outgoing = place_blocks(slot_of, wo_terms, owner_count * slot_count)
+    outgoing = place_blocks(slot_of, in_vmem(wo_terms), owner_count * slot_count)
     outgoing = outgoing.reshape(owner_count, slot_count, rows_dev, quarter)
     own_cols = lax.all_to_all(outgoing, "shard", 0, 0, tiled=True)
-    own_cols, factors, small_sum = lax.optimization_barrier((own_cols, factors, small_sum))
+    own_cols, factors = lax.optimization_barrier((own_cols, factors))
     own_cols = own_cols.transpose(1, 0, 2, 3).reshape(slot_count, side, quarter)
     gathered = lax.all_to_all(
         jnp.broadcast_to(own_cols[None], (ways,) + own_cols.shape), "tensor", 0, 0, tiled=True
     )
     update, row_new, col_new = precondition(
-        here.reshape(1).astype(jnp.int32), gathered, factors, row_moments.T, col_moments, rows_dev
+        here.reshape(1).astype(jnp.int32), in_vmem(gathered), factors, row_moments.T, col_moments, rows_dev
     )
     row_new = row_new.T
     returned = lax.all_to_all(update, "shard", 0, 0, tiled=True)
@@ -265,7 +269,7 @@
 
     wo_new, wo_low = apply_updates(
         slot_of,
-        returned.reshape(owner_count * slot_count, rows_dev, quarter),
+        in_vmem(returned.reshape(owner_count * slot_count, rows_dev, quarter)),
         wo_master.reshape(block_count, rows_dev, quarter),
         ways,
     )

time: 165 us -> 163 us (0.988)
  local copies, waits for them, and re-layouts: 14.5 us -> 7.59 us
  starting transfers between devices: 76.1 us -> 79.7 us
  waiting for transfers between devices: 54.3 us -> 56.9 us
    unnamed x59 -> x49, local copies, waits for them, and re-layouts: 9.4 us -> 4.07 us
    all_to_all x1, waiting for transfers between devices: 15.8 us -> 20.5 us  [per_device(): returned = lax.all_to_all(update, 'shard', 0, 0, tiled=True)]
    ppermute x9, starting transfers between devices: 29 us -> 31 us  [from_peers(): lax.ppermute(value, axis, [(i, (i + k) % count) for i in range(count)])]
    ppermute x9, waiting for transfers between devices: 22.9 us -> 20.9 us  [from_peers(): lax.ppermute(value, axis, [(i, (i + k) % count) for i in range(count)])]
  transfers between devices with their start and end apart: 14 -> 14, of which waited for: 7 -> 8; matrix products, arithmetic and copies ran while one was open for 9% -> 6% of each run, Pallas kernels for 3% -> 3%
where the time goes in v3:
time: 163 us; the launch traced here: 162 us
  starting transfers between devices  79.7 us (49%)
  waiting for transfers between devices  56.9 us (35%)
  Pallas kernels  10.3 us (6%)
  local copies, waits for them, and re-layouts  7.59 us (5%)
  other arithmetic  4.15 us (3%)
  matrix products  2.42 us (1%)
    ppermute x9, starting transfers between devices, from_peers(): lax.ppermute(value, axis, [(i, (i + k) % count) for i in range(count)])  31 us
    ppermute x9, waiting for transfers between devices, from_peers(): lax.ppermute(value, axis, [(i, (i + k) % count) for i in range(count)])  20.9 us
    all_to_all x1, waiting for transfers between devices, per_device(): returned = lax.all_to_all(update, 'shard', 0, 0, tiled=True)  20.5 us
    all_to_all x1, starting transfers between devices, per_device(): own_cols = lax.all_to_all(outgoing, 'shard', 0, 0, tiled=True)  19.3 us
    all_to_all x1, starting transfers between devices, per_device(): returned = lax.all_to_all(update, 'shard', 0, 0, tiled=True)  16.1 us
    all_to_all x1, waiting for transfers between devices, per_device(): wo_terms = lax.all_to_all(wo_parts, 'tensor', 0, 0, tiled=True)  8.77 us
    all_to_all x1, waiting for transfers between devices, per_device(): wo_low = lax.all_to_all(wo_low, 'tensor', 0, 0, tiled=True)  6.69 us
    all_to_all x1, starting transfers between devices, per_device(): lax.all_to_all(jnp.broadcast_to(own_cols[None], (ways,) + own_cols.shape)...  4.65 us
  transfers between devices with their start and end apart: 14, of which 8 were waited for; matrix products, arithmetic and copies ran while one was open for 6% of the time, Pallas kernels for 3%

profile of v3, /device:TPU:32, one launch (start us, length us, event | category | flops | bytes accessed | tf_op | source)
XLA Modules:
  0.0 162.2 jit_solution(4034571800539899422)
XLA Ops:
  0.6 2.0 %split_columns.1 = bf16[4,128,4,128]{3,2,1,0:T(4,128)(2,1)} custom-call(bf16[128,4,512]{2,1,0:T(4,128)(2,1)} %bitcast.68), custom_call_target="tpu_custom_call" | custom-call | tf_op jit(solution)/shard_map/split_columns/pallas_call | solution.py:41
  2.7 4.4 %all-to-all-start = ((bf16[4,128,4,128]{3,2,1,0:T(4,128)(2,1)}), bf16[4,128,4,128]{3,2,1,0:T(4,128)(2,1)S(1)}, u32[]{:S(2)}, u32[]{:S(2)}) async-start(bf16[4,128,4,128]{3,2,1,0:T(4,128)(2,1)} %split_columns.1), calls=%async_computation | async-start | bytes 1048576 | tf_op jit(solution)/shard_map/all_to_all | solution.py:215
  7.1 0.2 convert_reduce_fusion
  7.3 0.5 multiply_add_fusion.2.slot_of
  7.8 8.8 %all-to-all-done.terms = bf16[4,128,4,128]{3,2,1,0:T(4,128)(2,1)S(1)} async-done(((bf16[4,128,4,128]{3,2,1,0:T(4,128)(2,1)}), bf16[4,128,4,128]{3,2,1,0:T(4,128)(2,1)S(1)}, u32[]{:S(2)}, u32[]{:S(2)}) %all-to-all-start) | async-done | bytes 524320 | tf_op jit(solution)/shard_map/all_to_all | solution.py:215
  16.6 1.7 %place_blocks.1 = bf16[256,4,128]{2,1,0:T(4,128)(2,1)} custom-call(s32[128]{0:T(128)} %multiply_add_fusion.2.slot_of, bf16[4,128,4,128]{3,2,1,0:T(4,128)(2,1)S(1)} %all-to-all-done.terms), custom_call_target="tpu_custom_call" | custom-call | tf_op jit(solution)/shard_map/place_blocks/pallas_call | solution.py:66
  18.3 19.3 %all-to-all-start.1 = ((bf16[128,2,4,128]{3,2,1,0:T(4,128)(2,1)}), bf16[128,2,4,128]{3,2,1,0:T(4,128)(2,1)S(1)}, u32[]{:S(2)}, u32[]{:S(2)}) async-start(bf16[128,2,4,128]{3,2,1,0:T(4,128)(2,1)} %bitcast.67), calls=%async_computation.1 | async-start | bytes 524288 | tf_op jit(solution)/shard_map/all_to_all | solution.py:237
  37.6 0.0 copy-start.17
  37.6 0.6 copy-done.17
  38.3 0.1 reshape_squeeze.7
  38.4 0.2 reshape_squeeze.6
  38.6 0.1 fusion.1
  38.7 0.6 constant_dynamic-slice_fusion.2
  39.4 0.0 copy-start.9
  39.4 0.0 copy-start.8
  39.4 3.2 %collective-permute-start.5 = (bf16[40,1024]{1,0:T(8,128)(2,1)S(1)}, bf16[40,1024]{1,0:T(8,128)(2,1)S(1)}, u32[]{:S(2)}, u32[]{:S(2)}) collective-permute-start(bf16[40,1024]{1,0:T(8,128)(2,1)S(1)} %bitcast.80), channel_id=1, source_target_pairs={{0,3},{1,0},{2,1},{3,2},{4,7},{5,4},{6,5},{7,6},{8,11},{9,8},{10,9... | collective-permute-start | bytes 245768 | tf_op jit(solution)/shard_map/ppermute | solution.py:183
  42.7 3.4 %collective-permute-start.4 = (bf16[40,1024]{1,0:T(8,128)(2,1)S(1)}, bf16[40,1024]{1,0:T(8,128)(2,1)S(1)}, u32[]{:S(2)}, u32[]{:S(2)}) collective-permute-start(bf16[40,1024]{1,0:T(8,128)(2,1)S(1)} %bitcast.78), channel_id=1, source_target_pairs={{0,2},{1,3},{2,0},{3,1},{4,6},{5,7},{6,4},{7,5},{8,10},{9,11},{10,... | collective-permute-start | bytes 245768 | tf_op jit(solution)/shard_map/ppermute | solution.py:183
  46.1 1.9 %collective-permute-start.3 = (bf16[40,1024]{1,0:T(8,128)(2,1)S(1)}, bf16[40,1024]{1,0:T(8,128)(2,1)S(1)}, u32[]{:S(2)}, u32[]{:S(2)}) collective-permute-start(bf16[40,1024]{1,0:T(8,128)(2,1)S(1)} %bitcast.79), channel_id=1, source_target_pairs={{0,1},{1,2},{2,3},{3,0},{4,5},{5,6},{6,7},{7,4},{8,9},{9,10},{10,1... | collective-permute-start | bytes 245768 | tf_op jit(solution)/shard_map/ppermute | solution.py:183
  48.0 0.1 pad_maximum_fusion.own
  48.1 0.0 copy-start
  48.1 3.9 %collective-permute-start = (bf16[2,2,128,512]{3,2,1,0:T(8,128)(2,1)S(1)}, bf16[2,2,128,512]{3,2,1,0:T(8,128)(2,1)S(1)}, u32[]{:S(2)}, u32[]{:S(2)}) collective-permute-start(bf16[2,2,128,512]{3,2,1,0:T(8,128)(2,1)S(1)} %pad_maximum_fusion.own), channel_id=1, source_target_pairs={{0,1},{1,2},{2,3},{3,0},{4,5},{5,6},{6,7},{7,4},{8,9},{9,10},{10,1... | collective-permute-start | bytes 1572872 | tf_op jit(solution)/shard_map/ppermute | solution.py:183
  52.0 4.6 %collective-permute-start.1 = (bf16[2,2,128,512]{3,2,1,0:T(8,128)(2,1)S(1)}, bf16[2,2,128,512]{3,2,1,0:T(8,128)(2,1)S(1)}, u32[]{:S(2)}, u32[]{:S(2)}) collective-permute-start(bf16[2,2,128,512]{3,2,1,0:T(8,128)(2,1)S(1)} %pad_maximum_fusion.own), channel_id=1, source_target_pairs={{0,2},{1,3},{2,0},{3,1},{4,6},{5,7},{6,4},{7,5},{8,10},{9,11},{10,... | collective-permute-start | bytes 1572872 | tf_op jit(solution)/shard_map/ppermute | solution.py:183
  56.6 0.0 collective-permute-done.5
  56.6 3.4 %collective-permute-start.2 = (bf16[2,2,128,512]{3,2,1,0:T(8,128)(2,1)S(1)}, bf16[2,2,128,512]{3,2,1,0:T(8,128)(2,1)S(1)}, u32[]{:S(2)}, u32[]{:S(2)}) collective-permute-start(bf16[2,2,128,512]{3,2,1,0:T(8,128)(2,1)S(1)} %pad_maximum_fusion.own), channel_id=1, source_target_pairs={{0,3},{1,0},{2,1},{3,2},{4,7},{5,4},{6,5},{7,6},{8,11},{9,8},{10,9... | collective-permute-start | bytes 1572872 | tf_op jit(solution)/shard_map/ppermute | solution.py:183
  60.0 0.0 copy-start.13
  60.0 0.7 copy-done.13
  60.7 0.9 copy.68
  61.6 0.0 collective-permute-done.4
  61.6 0.0 collective-permute-done.3
  61.6 0.0 copy-start.11
  61.6 0.0 copy-start.12
  61.6 0.1 fusion.5
  61.7 0.8 copy-done.10
  62.5 0.1 copy-done.11
  62.6 0.1 copy-done.12
  62.6 0.8 fusion.12
  63.4 2.2 %collective-permute-done.rest_0_ = bf16[2,2,128,512]{3,2,1,0:T(8,128)(2,1)S(1)} collective-permute-done((bf16[2,2,128,512]{3,2,1,0:T(8,128)(2,1)S(1)}, bf16[2,2,128,512]{3,2,1,0:T(8,128)(2,1)S(1)}, u32[]{:S(2)}, u32[]{:S(2)}) %collective-permute-start) | collective-permute-done | bytes 524320 | tf_op jit(solution)/shard_map/ppermute | solution.py:183
  65.7 11.3 %collective-permute-done.1.rest_1_ = bf16[2,2,128,512]{3,2,1,0:T(8,128)(2,1)S(1)} collective-permute-done((bf16[2,2,128,512]{3,2,1,0:T(8,128)(2,1)S(1)}, bf16[2,2,128,512]{3,2,1,0:T(8,128)(2,1)S(1)}, u32[]{:S(2)}, u32[]{:S(2)}) %collective-permute-start.1) | collective-permute-done | bytes 524320 | tf_op jit(solution)/shard_map/ppermute | solution.py:183
  77.0 1.4 collective-permute-done.2.rest_2_
  78.4 0.1 copy.67
  78.5 1.1 broadcast_in_dim.5
  79.6 0.0 copy-start.15
  79.6 0.0 copy-start.16
  79.6 4.6 %all-to-all-start.2 = ((bf16[4,2,512,128]{3,2,1,0:T(8,128)(2,1)}), bf16[4,2,512,128]{3,2,1,0:T(8,128)(2,1)S(1)}, u32[]{:S(2)}, u32[]{:S(2)}) async-start(bf16[4,2,512,128]{3,2,1,0:T(8,128)(2,1)} %broadcast_in_dim.5), calls=%async_computation.2 | async-start | bytes 2097152 | tf_op jit(solution)/shard_map/all_to_all | solution.py:240
  84.3 0.6 fusion.14
  84.9 5.1 %collective-permute-start.6 = (bf16[40,1024]{1,0:T(8,128)(2,1)S(1)}, bf16[40,1024]{1,0:T(8,128)(2,1)S(1)}, u32[]{:S(2)}, u32[]{:S(2)}) collective-permute-start(bf16[40,1024]{1,0:T(8,128)(2,1)S(1)} %fusion.8), channel_id=1, source_target_pairs={{0,3},{1,0},{2,1},{3,2},{4,7},{5,4},{6,5},{7,6},{8,11},{9,8},{10,9... | collective-permute-start | bytes 245768 | tf_op jit(solution)/shard_map/ppermute | solution.py:183
  90.0 2.8 %collective-permute-start.7 = (bf16[40,1024]{1,0:T(8,128)(2,1)S(1)}, bf16[40,1024]{1,0:T(8,128)(2,1)S(1)}, u32[]{:S(2)}, u32[]{:S(2)}) collective-permute-start(bf16[40,1024]{1,0:T(8,128)(2,1)S(1)} %fusion.8), channel_id=1, source_target_pairs={{0,2},{1,3},{2,0},{3,1},{4,6},{5,7},{6,4},{7,5},{8,10},{9,11},{10,... | collective-permute-start | bytes 245768 | tf_op jit(solution)/shard_map/ppermute | solution.py:183
  92.8 2.8 %collective-permute-start.8 = (bf16[40,1024]{1,0:T(8,128)(2,1)S(1)}, bf16[40,1024]{1,0:T(8,128)(2,1)S(1)}, u32[]{:S(2)}, u32[]{:S(2)}) collective-permute-start(bf16[40,1024]{1,0:T(8,128)(2,1)S(1)} %fusion.8), channel_id=1, source_target_pairs={{0,1},{1,2},{2,3},{3,0},{4,5},{5,6},{6,7},{7,4},{8,9},{9,10},{10,1... | collective-permute-start | bytes 245768 | tf_op jit(solution)/shard_map/ppermute | solution.py:183
  95.6 5.2 %collective-permute-done.6 = bf16[40,1024]{1,0:T(8,128)(2,1)S(1)} collective-permute-done((bf16[40,1024]{1,0:T(8,128)(2,1)S(1)}, bf16[40,1024]{1,0:T(8,128)(2,1)S(1)}, u32[]{:S(2)}, u32[]{:S(2)}) %collective-permute-start.6) | collective-permute-done | bytes 81952 | tf_op jit(solution)/shard_map/ppermute | solution.py:183
  100.9 0.7 collective-permute-done.7
  101.6 4.4 %precondition.1 = (bf16[128,2,4,128]{3,2,1,0:T(4,128)(2,1)}, f32[512,2]{1,0:T(8,128)}, f32[2,512]{1,0:T(2,128)}) custom-call(s32[1]{0:T(128)} %bitcast.here, bf16[4,2,512,128]{3,2,1,0:T(8,128)(2,1)S(1)} %all-to-all-done.2.columns, bf16[2,2,128,512]{3,2,1,0:T(8,128)(2,1)} %copy-done, bf16[2,2,128,512]{3,2,1,0:T(8,128)(2,1)} %copy-done.3, ...), custom_call_target="tpu_custom_call" | custom-call | tf_op jit(solution)/shard_map/precondition/pallas_call | solution.py:119
  106.0 16.1 %all-to-all-start.3 = ((bf16[128,2,4,128]{3,2,1,0:T(4,128)(2,1)}), bf16[128,2,4,128]{3,2,1,0:T(4,128)(2,1)S(1)}, u32[]{:S(2)}, u32[]{:S(2)}) async-start(bf16[128,2,4,128]{3,2,1,0:T(4,128)(2,1)} %get-tuple-element.29), calls=%async_computation.3 | async-start | bytes 524288 | tf_op jit(solution)/shard_map/all_to_all | solution.py:247
  122.3 0.7 copy.85
  123.0 0.6 reshape.78
  123.6 0.5 copy.69
  124.1 20.5 %all-to-all-done.3 = bf16[128,2,4,128]{3,2,1,0:T(4,128)(2,1)S(1)} async-done(((bf16[128,2,4,128]{3,2,1,0:T(4,128)(2,1)}), bf16[128,2,4,128]{3,2,1,0:T(4,128)(2,1)S(1)}, u32[]{:S(2)}, u32[]{:S(2)}) %all-to-all-start.3) | async-done | bytes 262176 | tf_op jit(solution)/shard_map/all_to_all | solution.py:247
  144.6 2.2 %apply_updates.1 = (f32[128,4,128]{2,1,0:T(4,128)}, bf16[4,128,4,128]{3,2,1,0:T(4,128)(2,1)}) custom-call(s32[128]{0:T(128)} %multiply_add_fusion.2.slot_of, bf16[256,4,128]{2,1,0:T(4,128)(2,1)S(1)} %bitcast.59, f32[128,4,128]{2,1,0:T(4,128)} %bitcast.73), custom_call_target="tpu_custom_call" | custom-call | tf_op jit(solution)/shard_map/apply_updates/pallas_call | solution.py:148
  146.8 4.2 %all-to-all-start.4 = ((bf16[4,128,4,128]{3,2,1,0:T(4,128)(2,1)}), bf16[4,128,4,128]{3,2,1,0:T(4,128)(2,1)S(1)}, u32[]{:S(2)}, u32[]{:S(2)}) async-start(bf16[4,128,4,128]{3,2,1,0:T(4,128)(2,1)} %get-tuple-element.31), calls=%async_computation.4 | async-start | bytes 1048576 | tf_op jit(solution)/shard_map/all_to_all | solution.py:276
  151.0 1.1 convolution_add_fusion.1
  152.2 0.7 copy.76
  152.9 1.3 convolution_add_fusion
  154.2 6.7 %all-to-all-done.4 = bf16[4,128,4,128]{3,2,1,0:T(4,128)(2,1)S(1)} async-done(((bf16[4,128,4,128]{3,2,1,0:T(4,128)(2,1)}), bf16[4,128,4,128]{3,2,1,0:T(4,128)(2,1)S(1)}, u32[]{:S(2)}, u32[]{:S(2)}) %all-to-all-start.4) | async-done | bytes 524320 | tf_op jit(solution)/shard_map/all_to_all | solution.py:276
  160.9 0.2 fusion.16
  161.1 1.2 pad_maximum_fusion.1
  (42 shorter events, 0.3 us)
Async XLA Ops:
  2.7 4.4 %copy-start.18 = (s32[128]{0:T(128)S(1)}, s32[128]{0:T(128)}, u32[]{:S(2)}) copy-start(s32[128]{0:T(128)} %param.25) | copy-start | bytes 1540
  2.7 13.9 %all-to-all-start = ((bf16[4,128,4,128]{3,2,1,0:T(4,128)(2,1)}), bf16[4,128,4,128]{3,2,1,0:T(4,128)(2,1)S(1)}, u32[]{:S(2)}, u32[]{:S(2)}) async-start(bf16[4,128,4,128]{3,2,1,0:T(4,128)(2,1)} %split_columns.1), calls=%async_computation | async-start | bytes 1048576 | tf_op jit(solution)/shard_map/all_to_all | solution.py:215
  18.3 20.1 %copy-start.6 = (bf16[1,32,4096]{2,1,0:T(8,128)(2,1)S(1)}, bf16[1,32,4096]{2,1,0:T(8,128)(2,1)}, u32[]{:S(2)}) copy-start(bf16[1,32,4096]{2,1,0:T(8,128)(2,1)} %param.26) | copy-start | bytes 786436
  18.3 60.1 %all-to-all-start.1 = ((bf16[128,2,4,128]{3,2,1,0:T(4,128)(2,1)}), bf16[128,2,4,128]{3,2,1,0:T(4,128)(2,1)S(1)}, u32[]{:S(2)}, u32[]{:S(2)}) async-start(bf16[128,2,4,128]{3,2,1,0:T(4,128)(2,1)} %bitcast.67), calls=%async_computation.1 | async-start | bytes 524288 | tf_op jit(solution)/shard_map/all_to_all | solution.py:237
  37.6 0.7 copy-start.17
  39.4 8.7 %copy-start.9 = (bf16[2,128,512]{2,1,0:T(8,128)(2,1)S(1)}, bf16[2,128,512]{2,1,0:T(8,128)(2,1)}, u32[]{:S(2)}) copy-start(bf16[2,128,512]{2,1,0:T(8,128)(2,1)} %param.21) | copy-start | bytes 786436
  39.4 8.6 %copy-start.8 = (bf16[2,128,512]{2,1,0:T(8,128)(2,1)S(1)}, bf16[2,128,512]{2,1,0:T(8,128)(2,1)}, u32[]{:S(2)}) copy-start(bf16[2,128,512]{2,1,0:T(8,128)(2,1)} %param.22) | copy-start | bytes 786436
  39.4 17.2 %collective-permute-start.5 = (bf16[40,1024]{1,0:T(8,128)(2,1)S(1)}, bf16[40,1024]{1,0:T(8,128)(2,1)S(1)}, u32[]{:S(2)}, u32[]{:S(2)}) collective-permute-start(bf16[40,1024]{1,0:T(8,128)(2,1)S(1)} %bitcast.80), channel_id=1, source_target_pairs={{0,3},{1,0},{2,1},{3,2},{4,7},{5,4},{6,5},{7,6},{8,11},{9,8},{10,9... | collective-permute-start | bytes 245768 | tf_op jit(solution)/shard_map/ppermute | solution.py:183
  42.7 18.9 %collective-permute-start.4 = (bf16[40,1024]{1,0:T(8,128)(2,1)S(1)}, bf16[40,1024]{1,0:T(8,128)(2,1)S(1)}, u32[]{:S(2)}, u32[]{:S(2)}) collective-permute-start(bf16[40,1024]{1,0:T(8,128)(2,1)S(1)} %bitcast.78), channel_id=1, source_target_pairs={{0,2},{1,3},{2,0},{3,1},{4,6},{5,7},{6,4},{7,5},{8,10},{9,11},{10,... | collective-permute-start | bytes 245768 | tf_op jit(solution)/shard_map/ppermute | solution.py:183
  46.1 15.5 %collective-permute-start.3 = (bf16[40,1024]{1,0:T(8,128)(2,1)S(1)}, bf16[40,1024]{1,0:T(8,128)(2,1)S(1)}, u32[]{:S(2)}, u32[]{:S(2)}) collective-permute-start(bf16[40,1024]{1,0:T(8,128)(2,1)S(1)} %bitcast.79), channel_id=1, source_target_pairs={{0,1},{1,2},{2,3},{3,0},{4,5},{5,6},{6,7},{7,4},{8,9},{9,10},{10,1... | collective-permute-start | bytes 245768 | tf_op jit(solution)/shard_map/ppermute | solution.py:183
  48.1 15.3 %copy-start = (bf16[2,2,128,512]{3,2,1,0:T(8,128)(2,1)}, bf16[2,2,128,512]{3,2,1,0:T(8,128)(2,1)S(1)}, u32[]{:S(2)}) copy-start(bf16[2,2,128,512]{3,2,1,0:T(8,128)(2,1)S(1)} %pad_maximum_fusion.own) | copy-start | bytes 1572868
  48.1 17.6 %collective-permute-start = (bf16[2,2,128,512]{3,2,1,0:T(8,128)(2,1)S(1)}, bf16[2,2,128,512]{3,2,1,0:T(8,128)(2,1)S(1)}, u32[]{:S(2)}, u32[]{:S(2)}) collective-permute-start(bf16[2,2,128,512]{3,2,1,0:T(8,128)(2,1)S(1)} %pad_maximum_fusion.own), channel_id=1, source_target_pairs={{0,1},{1,2},{2,3},{3,0},{4,5},{5,6},{6,7},{7,4},{8,9},{9,10},{10,1... | collective-permute-start | bytes 1572872 | tf_op jit(solution)/shard_map/ppermute | solution.py:183
  52.0 25.0 %collective-permute-start.1 = (bf16[2,2,128,512]{3,2,1,0:T(8,128)(2,1)S(1)}, bf16[2,2,128,512]{3,2,1,0:T(8,128)(2,1)S(1)}, u32[]{:S(2)}, u32[]{:S(2)}) collective-permute-start(bf16[2,2,128,512]{3,2,1,0:T(8,128)(2,1)S(1)} %pad_maximum_fusion.own), channel_id=1, source_target_pairs={{0,2},{1,3},{2,0},{3,1},{4,6},{5,7},{6,4},{7,5},{8,10},{9,11},{10,... | collective-permute-start | bytes 1572872 | tf_op jit(solution)/shard_map/ppermute | solution.py:183
  56.6 21.7 %collective-permute-start.2 = (bf16[2,2,128,512]{3,2,1,0:T(8,128)(2,1)S(1)}, bf16[2,2,128,512]{3,2,1,0:T(8,128)(2,1)S(1)}, u32[]{:S(2)}, u32[]{:S(2)}) collective-permute-start(bf16[2,2,128,512]{3,2,1,0:T(8,128)(2,1)S(1)} %pad_maximum_fusion.own), channel_id=1, source_target_pairs={{0,3},{1,0},{2,1},{3,2},{4,7},{5,4},{6,5},{7,6},{8,11},{9,8},{10,9... | collective-permute-start | bytes 1572872 | tf_op jit(solution)/shard_map/ppermute | solution.py:183
  60.0 0.7 copy-start.13
  61.6 0.9 copy-start.10
  61.6 1.0 copy-start.11
  61.6 1.0 copy-start.12
  65.7 13.9 %copy-start.3 = (bf16[2,2,128,512]{3,2,1,0:T(8,128)(2,1)}, bf16[2,2,128,512]{3,2,1,0:T(8,128)(2,1)S(1)}, u32[]{:S(2)}) copy-start(bf16[2,2,128,512]{3,2,1,0:T(8,128)(2,1)S(1)} %collective-permute-done.rest_0_) | copy-start | bytes 1572868
  77.0 2.6 %copy-start.4 = (bf16[2,2,128,512]{3,2,1,0:T(8,128)(2,1)}, bf16[2,2,128,512]{3,2,1,0:T(8,128)(2,1)S(1)}, u32[]{:S(2)}) copy-start(bf16[2,2,128,512]{3,2,1,0:T(8,128)(2,1)S(1)} %collective-permute-done.1.rest_1_) | copy-start | bytes 1572868
  78.4 1.2 copy-start.5
  79.6 4.7 %copy-start.14 = (f32[2,8]{1,0:T(2,128)S(1)}, f32[2,8]{1,0:T(2,128)}, u32[]{:S(2)}) copy-start(f32[2,8]{1,0:T(2,128)} %param.31) | copy-start | bytes 196
  79.6 4.7 %copy-start.15 = (f32[2,8]{1,0:T(2,128)S(1)}, f32[2,8]{1,0:T(2,128)}, u32[]{:S(2)}) copy-start(f32[2,8]{1,0:T(2,128)} %param.32) | copy-start | bytes 196
  79.6 4.7 %copy-start.16 = (f32[2,8]{1,0:T(2,128)S(1)}, f32[2,8]{1,0:T(2,128)}, u32[]{:S(2)}) copy-start(f32[2,8]{1,0:T(2,128)} %param.33) | copy-start | bytes 196
  79.6 22.0 %all-to-all-start.2 = ((bf16[4,2,512,128]{3,2,1,0:T(8,128)(2,1)}), bf16[4,2,512,128]{3,2,1,0:T(8,128)(2,1)S(1)}, u32[]{:S(2)}, u32[]{:S(2)}) async-start(bf16[4,2,512,128]{3,2,1,0:T(8,128)(2,1)} %broadcast_in_dim.5), calls=%async_computation.2 | async-start | bytes 2097152 | tf_op jit(solution)/shard_map/all_to_all | solution.py:240
  84.9 16.0 %collective-permute-start.6 = (bf16[40,1024]{1,0:T(8,128)(2,1)S(1)}, bf16[40,1024]{1,0:T(8,128)(2,1)S(1)}, u32[]{:S(2)}, u32[]{:S(2)}) collective-permute-start(bf16[40,1024]{1,0:T(8,128)(2,1)S(1)} %fusion.8), channel_id=1, source_target_pairs={{0,3},{1,0},{2,1},{3,2},{4,7},{5,4},{6,5},{7,6},{8,11},{9,8},{10,9... | collective-permute-start | bytes 245768 | tf_op jit(solution)/shard_map/ppermute | solution.py:183
  90.0 11.5 %collective-permute-start.7 = (bf16[40,1024]{1,0:T(8,128)(2,1)S(1)}, bf16[40,1024]{1,0:T(8,128)(2,1)S(1)}, u32[]{:S(2)}, u32[]{:S(2)}) collective-permute-start(bf16[40,1024]{1,0:T(8,128)(2,1)S(1)} %fusion.8), channel_id=1, source_target_pairs={{0,2},{1,3},{2,0},{3,1},{4,6},{5,7},{6,4},{7,5},{8,10},{9,11},{10,... | collective-permute-start | bytes 245768 | tf_op jit(solution)/shard_map/ppermute | solution.py:183
  92.8 29.3 %collective-permute-start.8 = (bf16[40,1024]{1,0:T(8,128)(2,1)S(1)}, bf16[40,1024]{1,0:T(8,128)(2,1)S(1)}, u32[]{:S(2)}, u32[]{:S(2)}) collective-permute-start(bf16[40,1024]{1,0:T(8,128)(2,1)S(1)} %fusion.8), channel_id=1, source_target_pairs={{0,1},{1,2},{2,3},{3,0},{4,5},{5,6},{6,7},{7,4},{8,9},{9,10},{10,1... | collective-permute-start | bytes 245768 | tf_op jit(solution)/shard_map/ppermute | solution.py:183
  106.0 38.6 %all-to-all-start.3 = ((bf16[128,2,4,128]{3,2,1,0:T(4,128)(2,1)}), bf16[128,2,4,128]{3,2,1,0:T(4,128)(2,1)S(1)}, u32[]{:S(2)}, u32[]{:S(2)}) async-start(bf16[128,2,4,128]{3,2,1,0:T(4,128)(2,1)} %get-tuple-element.29), calls=%async_computation.3 | async-start | bytes 524288 | tf_op jit(solution)/shard_map/all_to_all | solution.py:247
  146.8 4.2 %copy-start.1 = (f32[2,128,512]{2,1,0:T(8,128)S(1)}, f32[2,128,512]{2,1,0:T(8,128)}, u32[]{:S(2)}) copy-start(f32[2,128,512]{2,1,0:T(8,128)} %param.19) | copy-start | bytes 1572868
  146.8 14.0 %all-to-all-start.4 = ((bf16[4,128,4,128]{3,2,1,0:T(4,128)(2,1)}), bf16[4,128,4,128]{3,2,1,0:T(4,128)(2,1)S(1)}, u32[]{:S(2)}, u32[]{:S(2)}) async-start(bf16[4,128,4,128]{3,2,1,0:T(4,128)(2,1)} %get-tuple-element.31), calls=%async_computation.4 | async-start | bytes 1048576 | tf_op jit(solution)/shard_map/all_to_all | solution.py:276
  151.0 1.2 copy-start.7
  151.0 1.9 %copy-start.2 = (f32[2,128,512]{2,1,0:T(8,128)S(1)}, f32[2,128,512]{2,1,0:T(8,128)}, u32[]{:S(2)}) copy-start(f32[2,128,512]{2,1,0:T(8,128)} %param.20) | copy-start | bytes 1572868
